TPU v7x, 256 devices: a whole 4x4x8 slice. The times are simulated.
256 devices in a mesh: gx: 4 (over x), gy: 8 (over y, z_lo), gz: 8 (over z_hi, core).
Axes of the slice: x: 4, y: 4, z: 8 (z_hi: 4, z_lo: 2; z = z_hi * 2 + z_lo), core: 2. Of those that a mesh axis runs over, the one named last changes fastest.
Arguments:
- features: bfloat16 [4, 8, 16, 128, 128], P('gx', 'gy', 'gz'), may hold values from -6 to 6
- positions: int32 [3, 4, 8, 16, 128], P(None, 'gx', 'gy', 'gz'), may hold values from 0 to 63
- wavevectors: int32 [3, 1024], replicated, may hold values from -6 to 6
- radial_mix: bfloat16 [768, 128], replicated, may hold values from -0.0546875 to 0.0546875
- charge_weight: bfloat16 [128, 128], replicated, may hold values from -0.5 to 0.5
- filters: float32 [1024, 128], replicated, may hold values from 0.01 to 0.1
- mix_weight: float32 [128, 128], replicated, may hold values from -0.5 to 0.5
- norm_gain: float32 [128], replicated, may hold values from 0.1 to 1.9
- up_weight: bfloat16 [128, 256], replicated, may hold values from -0.5 to 0.5
- down_weight: bfloat16 [256, 128], replicated, may hold values from -0.375 to 0.375
Outputs:
- updated: bfloat16 [4, 8, 16, 128, 128], P('gx', 'gy', 'gz')
All inputs are finite; a program needn't handle non-finite values.
Results may differ from a plain program's by a relative error of at most 0.006.
Values may be sent and summed in bfloat16 or wider, within the bound.
A program may use at most 64 MiB of HBM per device.

v0:
```python
import math

import jax
import jax.numpy as jnp
from jax import lax
from jax.sharding import PartitionSpec as P

NRBF = 6
GRID = 64


SHARP = 18.0
TWO_PI = 2.0 * math.pi
EPS = 1e-06
CONTRACT_FIRST = (((0,), (0,)), ((), ()))


def extended(array, sides, width):
    for axis, dim in sides:
        size, length = (lax.axis_size(axis), array.shape[dim])
        up = [(i, (i + 1) % size) for i in range(size)]
        down = [(j, i) for i, j in up]
        last = lax.slice_in_dim(array, length - width, length, axis=dim)
        first = lax.slice_in_dim(array, 0, width, axis=dim)
        before = lax.ppermute(last, axis, up)
        after = lax.ppermute(first, axis, down)
        array = jnp.concatenate([before, array, after], axis=dim)
    return array


def radial_basis(center, nearby_pos):
    tile_size = center.shape[1]
    offsets = (
        jnp.stack(
            [lax.broadcasted_iota(jnp.int32, (3, 3, 3, 1), component) for component in range(3)]
        )
        - 1
    )
    coords = (nearby_pos + offsets * GRID).reshape(3, 27 * tile_size)
    displace = coords[:, None, :] - center[:, :, None]
    square = jnp.sum(displace * displace, axis=0)
    scaled_dist = jnp.sqrt(square.astype(jnp.float32)) / GRID
    inside = (square > 0) & (square < GRID * GRID)
    envelope = jnp.where(inside, (1.0 - scaled_dist * scaled_dist) ** 2, 0.0)
    centres = (jnp.arange(NRBF, dtype=jnp.float32) + 0.5) / NRBF
    radial = (
        jnp.exp(-SHARP * (scaled_dist[:, None, :] - centres[None, :, None]) ** 2)
        * envelope[:, None, :]
    )
    return radial.astype(jnp.bfloat16)


def phase_tables(wavevectors, coords, lengths):
    fraction = jnp.zeros((wavevectors.shape[1], coords.shape[1]), jnp.float32)
    for component in range(3):
        product = jnp.mod(
            wavevectors[component][:, None] * coords[component][None, :], lengths[component]
        )
        fraction = fraction + product.astype(jnp.float32) / lengths[component]
    phase_angle = TWO_PI * fraction
    return (jnp.cos(phase_angle).astype(jnp.bfloat16), jnp.sin(phase_angle).astype(jnp.bfloat16))


def filter_mix(filters, factor, mix_weight):
    return jnp.dot(filters * factor, mix_weight, precision=lax.Precision.HIGHEST).astype(
        jnp.bfloat16
    )


def on_device(
    features,
    positions,
    wavevectors,
    radial_mix,
    charge_weight,
    filters,
    mix_weight,
    norm_gain,
    up_weight,
    down_weight,
):
    count_x, count_y, count_z, tile_size, feat_width = features.shape
    beside_all = extended(features, (("gx", 0), ("gy", 1), ("gz", 2)), 1)
    around_pos = extended(positions, (("gx", 1), ("gy", 2), ("gz", 3)), 1)
    anchor = jnp.zeros((), jnp.int32)

    def one_tile(flat_index):
        tile_x = flat_index // (count_y * count_z)
        tile_y = flat_index // count_z % count_y
        tile_z = flat_index % count_z
        neighbour = lax.dynamic_slice(
            beside_all, (tile_x, tile_y, tile_z, anchor, anchor), (3, 3, 3, tile_size, feat_width)
        )
        nearby_pos = lax.dynamic_slice(
            around_pos, (anchor, tile_x, tile_y, tile_z, anchor), (3, 3, 3, 3, tile_size)
        )
        center = lax.dynamic_slice(
            positions, (anchor, tile_x, tile_y, tile_z, anchor), (3, 1, 1, 1, tile_size)
        ).reshape(3, tile_size)
        radial = radial_basis(center, nearby_pos)
        pooled = jnp.einsum(
            "irj,jd->ird",
            radial,
            neighbour.reshape(27 * tile_size, feat_width),
            preferred_element_type=jnp.float32,
        )
        pooled = pooled.astype(jnp.bfloat16).reshape(tile_size, -1)
        return jnp.dot(pooled, radial_mix, preferred_element_type=jnp.float32)

    message = lax.map(one_tile, jnp.arange(count_x * count_y * count_z, dtype=jnp.int32))
    message = message.reshape(count_x * count_y * count_z * tile_size, feat_width)
    atom_count = count_x * count_y * count_z * tile_size
    counts = (count_x, count_y, count_z)
    axis_sizes = (lax.axis_size("gx"), lax.axis_size("gy"), lax.axis_size("gz"))
    axis_index = (lax.axis_index("gx"), lax.axis_index("gy"), lax.axis_index("gz"))
    lengths = tuple((counts[component] * axis_sizes[component] * GRID for component in range(3)))
    coords = jnp.stack(
        [
            (
                axis_index[component] * counts[component]
                + lax.broadcasted_iota(jnp.int32, (count_x, count_y, count_z, tile_size), component)
            )
            * GRID
            + positions[component]
            for component in range(3)
        ]
    ).reshape(3, atom_count)
    cos_table, sin_table = phase_tables(wavevectors, coords, lengths)
    charges = jnp.dot(
        features.reshape(atom_count, feat_width), charge_weight, preferred_element_type=jnp.float32
    ).astype(jnp.bfloat16)
    partial_cos = jnp.dot(cos_table, charges, preferred_element_type=jnp.float32)
    partial_sin = jnp.dot(sin_table, charges, preferred_element_type=jnp.float32)
    scale = 1.0 / math.sqrt(atom_count * axis_sizes[0] * axis_sizes[1] * axis_sizes[2])
    summed_cos, summed_sin = lax.psum((partial_cos, partial_sin), ("gx", "gy", "gz"))
    filtered_cos = filter_mix(filters, summed_cos * scale, mix_weight)
    filtered_sin = filter_mix(filters, summed_sin * scale, mix_weight)
    longrange = lax.dot_general(
        cos_table, filtered_cos, CONTRACT_FIRST, preferred_element_type=jnp.float32
    )
    longrange = longrange + lax.dot_general(
        sin_table, filtered_sin, CONTRACT_FIRST, preferred_element_type=jnp.float32
    )
    flat_sum = features.reshape(atom_count, feat_width).astype(jnp.float32) + message + longrange
    normed = (
        flat_sum
        * lax.rsqrt(jnp.mean(flat_sum * flat_sum, axis=-1, keepdims=True) + EPS)
        * norm_gain
    )
    hidden = jax.nn.silu(
        jnp.dot(normed.astype(jnp.bfloat16), up_weight, preferred_element_type=jnp.float32)
    ).astype(jnp.bfloat16)
    updated = flat_sum + jnp.dot(hidden, down_weight, preferred_element_type=jnp.float32)
    return updated.reshape(features.shape).astype(jnp.bfloat16)


def solution(mesh):
    in_specs = (
        P("gx", "gy", "gz", None, None),
        P(None, "gx", "gy", "gz", None),
        P(),
        P(),
        P(),
        P(),
        P(),
        P(),
        P(),
        P(),
    )
    out_specs = P("gx", "gy", "gz", None, None)
    return jax.shard_map(
        on_device, mesh=mesh, in_specs=in_specs, out_specs=out_specs, check_vma=False
    )
```

profile of v0, /device:TPU:1, one launch (start us, length us, event | category | flops | bytes accessed | tf_op | source)
XLA Modules:
  0.0 329.9 jit_solution(6805383220213072377)
XLA Ops:
  6.5 2.0 collective-permute-start
  8.6 1.3 collective-permute-start.1
  10.0 2.5 collective-permute-start.7
  13.4 1.0 convolution_convert_fusion.2
  15.1 6.5 %fusion.25 = f32[1024,128]{1,0:T(8,128)} fusion(bf16[256,128]{1,0:T(8,128)(2,1)S(1)} %convolution_convert_fusion.2, s32[256]{0:T(256)S(1)} %get-tuple-element.130, s32[1024]{0:T(1024)S(1)} %bitcast.63, s32[256]{0:T(256)S(1)} %get-tuple-element.131, s32[1024]{0:T(1024)S(1)} %bitcast.67, s32[256]{0:T(256)S(1)} %get-tuple-element.129, s32[1024]{0:T(1024)S(1)} %bitcast.59), kind=kOutput, calls=%fused_computation.60 | convolution fusion | flops 79167488 | bytes 605184 | tf_op jit(solution)/shard_map/dot_general | solution.py:132
  21.7 4.4 %collective-permute-start.3 = (s32[3,3,1,2,128]{4,3,2,1,0:T(2,128)S(1)}, s32[3,3,1,2,128]{4,3,2,1,0:T(2,128)S(1)}, u32[]{:S(2)}, u32[]{:S(2)}) collective-permute-start(s32[3,3,1,2,128]{4,3,2,1,0:T(2,128)S(1)} %constant_dynamic-update-slice_fusion), channel_id=1, source_target_pairs={{8,0},{16,8},{24,16},{32,24},{40,32},{48,40},{56,48},{0,56},{9,1},... | collective-permute-start | bytes 27656 | tf_op jit(solution)/shard_map/ppermute | solution.py:26
  26.1 6.5 %fusion.23 = f32[1024,128]{1,0:T(8,128)} fusion(bf16[256,128]{1,0:T(8,128)(2,1)S(1)} %convolution_convert_fusion.2, s32[256]{0:T(256)S(1)} %get-tuple-element.130, s32[1024]{0:T(1024)S(1)} %bitcast.64, s32[256]{0:T(256)S(1)} %get-tuple-element.131, s32[1024]{0:T(1024)S(1)} %bitcast.68, s32[256]{0:T(256)S(1)} %get-tuple-element.129, s32[1024]{0:T(1024)S(1)} %bitcast.60), kind=kOutput, calls=%fused_computation.58 | convolution fusion | flops 79167488 | bytes 605184 | tf_op jit(solution)/shard_map/dot_general | solution.py:133
  32.7 3.6 %collective-permute-start.9 = (bf16[3,1,2,128,128]{4,3,2,1,0:T(8,128)(2,1)S(1)}, bf16[3,1,2,128,128]{4,3,2,1,0:T(8,128)(2,1)S(1)}, u32[]{:S(2)}, u32[]{:S(2)}) collective-permute-start(bf16[3,1,2,128,128]{4,3,2,1,0:T(8,128)(2,1)S(1)} %constant_dynamic-update-slice_fusion.3), channel_id=1, source_target_pairs={{8,0},{16,8},{24,16},{32,24},{40,32},{48,40},{56,48},{0,56},{9,1},... | collective-permute-start | bytes 589832 | tf_op jit(solution)/shard_map/ppermute | solution.py:26
  36.4 2.7 collective-permute-start.5
  39.1 3.0 collective-permute-start.4
  42.1 1.4 collective-permute-done.5
  43.5 1.2 collective-permute-done.8
  44.9 4.7 %collective-permute-start.11 = (bf16[3,3,1,128,128]{4,3,2,1,0:T(8,128)(2,1)S(1)}, bf16[3,3,1,128,128]{4,3,2,1,0:T(8,128)(2,1)S(1)}, u32[]{:S(2)}, u32[]{:S(2)}) collective-permute-start(bf16[3,3,1,128,128]{4,3,2,1,0:T(8,128)(2,1)S(1)} %get-tuple-element.123), channel_id=1, source_target_pairs={{1,0},{2,1},{3,2},{4,3},{5,4},{6,5},{7,6},{0,7},{9,8},{10,9},{11,1... | collective-permute-start | bytes 884744 | tf_op jit(solution)/shard_map/ppermute | solution.py:26
  50.3 242.3 %all-reduce.3.cloned.1.call-done = (f32[1024,128]{1,0:T(8,128)}, f32[1024,128]{1,0:T(8,128)}) async-done(((f32[1024,128]{1,0:T(8,128)}, f32[1024,128]{1,0:T(8,128)}), (f32[1024,128]{1,0:T(8,128)}, f32[1024,128]{1,0:T(8,128)})) %all-reduce.3.cloned.1.call-update) | async-done | bytes 1048592 | tf_op jit(solution)/shard_map/psum | solution.py:135
  292.6 1.6 convolution_convert_fusion.1
  294.3 5.2 %fusion.24 = f32[256,128]{1,0:T(8,128)S(1)} fusion(bf16[1024,128]{1,0:T(8,128)(2,1)S(1)} %convolution_convert_fusion.1, s32[256]{0:T(256)S(1)} %get-tuple-element.130, s32[1024]{0:T(1024)S(1)} %bitcast.65, s32[256]{0:T(256)S(1)} %get-tuple-element.131, s32[1024]{0:T(1024)S(1)} %bitcast.69, s32[256]{0:T(256)S(1)} %get-tuple-element.129, s32[1024]{0:T(1024)S(1)} %bitcast.61), kind=kOutput, calls=%fused_computation.59 | convolution fusion | flops 79167488 | bytes 408576 | tf_op jit(solution)/shard_map/dot_general | solution.py:138
  299.5 1.3 convolution_convert_fusion
  301.0 15.6 %while.12 = (s32[]{:T(128)}, f32[2,128,128]{2,1,0:T(8,128)S(1)}, s32[2]{0:T(128)S(1)}, s32[3,3,3,4,128]{4,3,2,1,0:T(4,128)S(1)}, s32[3,1,1,2,128]{4,3,2,1,0:T(2,...) while((s32[]{:T(128)}, f32[2,128,128]{2,1,0:T(8,128)S(1)}, ...), condition=%wide.region_2.3_spmd, body=%wide.region_0.2_spmd.sunk | while | flops 725543424 | bytes 14143097 | solution.py:110
  304.8 0.9 sqrt_multiply_fusion.2
  305.7 2.9 fusion.106
  312.5 0.9 sqrt_multiply_fusion.2
  313.4 2.9 fusion.106
  316.7 5.3 %multiply_reduce_fusion.1 = (f32[256]{0:T(256)S(1)}, f32[256,128]{1,0:T(8,128)S(1)}) fusion(f32[256,128]{1,0:T(8,128)S(1)} %bitcast_add_fusion, f32[256,128]{1,0:T(8,128)S(1)} %fusion.24, bf16[1024,128]{1,0:T(8,128)(2,1)S(1)} %copy-done.5, s32[256]{0:T(256)S(1)} %get-tuple-element.130, s32[1024]{0:T(1024)S(1)} %bitcast.66, s32[256]{0:T(256)S(1)} %get-tuple-element.131, ...), kind=kOutput, calls=%fused_computation.67 | convolution fusion | flops 79298304 | bytes 671744 | tf_op jit(solution)/shard_map/dot_general | solution.py:141
  322.0 1.0 fusion.6
  (81 shorter events, 6.7 us)
Async XLA Ops:
  6.5 286.1 %copy-start = (f32[128,128]{1,0:T(8,128)S(1)}, f32[128,128]{1,0:T(8,128)}, u32[]{:S(2)}) copy-start(f32[128,128]{1,0:T(8,128)} %param.18) | copy-start | bytes 196612
  6.5 286.1 %all-reduce.3.cloned.1.call-start = ((), (), s32[]{:S(2)}) async-start(), calls=%async_computation | async-start | bytes 2097152 | tf_op jit(solution)/shard_map/psum | solution.py:135
  6.5 15.1 %collective-permute-start = (s32[3,1,1,2,128]{4,3,2,1,0:T(2,128)}, s32[3,1,1,2,128]{4,3,2,1,0:T(2,128)S(1)}, u32[]{:S(2)}, u32[]{:S(2)}) collective-permute-start(s32[3,1,1,2,128]{4,3,2,1,0:T(2,128)} %param.13), channel_id=1, source_target_pairs={{0,64},{64,128},{128,192},{192,0},{1,65},{65,129},{129,193},{193,1... | collective-permute-start | bytes 9224 | tf_op jit(solution)/shard_map/ppermute | solution.py:25
  8.6 13.1 %collective-permute-start.1 = (s32[3,1,1,2,128]{4,3,2,1,0:T(2,128)}, s32[3,1,1,2,128]{4,3,2,1,0:T(2,128)S(1)}, u32[]{:S(2)}, u32[]{:S(2)}) collective-permute-start(s32[3,1,1,2,128]{4,3,2,1,0:T(2,128)} %param.13), channel_id=1, source_target_pairs={{64,0},{128,64},{192,128},{0,192},{65,1},{129,65},{193,129},{1,193... | collective-permute-start | bytes 9224 | tf_op jit(solution)/shard_map/ppermute | solution.py:26
  9.8 22.8 %collective-permute-start.6 = (bf16[1,1,2,128,128]{4,3,2,1,0:T(8,128)(2,1)}, bf16[1,1,2,128,128]{4,3,2,1,0:T(8,128)(2,1)S(1)}, u32[]{:S(2)}, u32[]{:S(2)}) collective-permute-start(bf16[1,1,2,128,128]{4,3,2,1,0:T(8,128)(2,1)} %param.12), channel_id=1, source_target_pairs={{0,64},{64,128},{128,192},{192,0},{1,65},{65,129},{129,193},{193,1... | collective-permute-start | bytes 196616 | tf_op jit(solution)/shard_map/ppermute | solution.py:25
  10.0 22.6 %collective-permute-start.7 = (bf16[1,1,2,128,128]{4,3,2,1,0:T(8,128)(2,1)}, bf16[1,1,2,128,128]{4,3,2,1,0:T(8,128)(2,1)S(1)}, u32[]{:S(2)}, u32[]{:S(2)}) collective-permute-start(bf16[1,1,2,128,128]{4,3,2,1,0:T(8,128)(2,1)} %param.12), channel_id=1, source_target_pairs={{64,0},{128,64},{192,128},{0,192},{65,1},{129,65},{193,129},{1,193... | collective-permute-start | bytes 196616 | tf_op jit(solution)/shard_map/ppermute | solution.py:26
  15.1 6.5 %copy-start.6 = (s32[3,1,1,2,128]{4,3,2,1,0:T(2,128)S(1)}, s32[3,1,1,2,128]{4,3,2,1,0:T(2,128)}, u32[]{:S(2)}) copy-start(s32[3,1,1,2,128]{4,3,2,1,0:T(2,128)} %param.13) | copy-start | bytes 9220
  21.7 11.0 %copy-start.3 = (bf16[1,1,2,128,128]{4,3,2,1,0:T(8,128)(2,1)S(1)}, bf16[1,1,2,128,128]{4,3,2,1,0:T(8,128)(2,1)}, u32[]{:S(2)}) copy-start(bf16[1,1,2,128,128]{4,3,2,1,0:T(8,128)(2,1)} %param.12) | copy-start | bytes 196612
  21.7 10.9 %collective-permute-start.3 = (s32[3,3,1,2,128]{4,3,2,1,0:T(2,128)S(1)}, s32[3,3,1,2,128]{4,3,2,1,0:T(2,128)S(1)}, u32[]{:S(2)}, u32[]{:S(2)}) collective-permute-start(s32[3,3,1,2,128]{4,3,2,1,0:T(2,128)S(1)} %constant_dynamic-update-slice_fusion), channel_id=1, source_target_pairs={{8,0},{16,8},{24,16},{32,24},{40,32},{48,40},{56,48},{0,56},{9,1},... | collective-permute-start | bytes 27656 | tf_op jit(solution)/shard_map/ppermute | solution.py:26
  26.0 6.6 %collective-permute-start.2 = (s32[3,3,1,2,128]{4,3,2,1,0:T(2,128)S(1)}, s32[3,3,1,2,128]{4,3,2,1,0:T(2,128)S(1)}, u32[]{:S(2)}, u32[]{:S(2)}) collective-permute-start(s32[3,3,1,2,128]{4,3,2,1,0:T(2,128)S(1)} %constant_dynamic-update-slice_fusion), channel_id=1, source_target_pairs={{0,8},{8,16},{16,24},{24,32},{32,40},{40,48},{48,56},{56,0},{1,9},... | collective-permute-start | bytes 27656 | tf_op jit(solution)/shard_map/ppermute | solution.py:25
  32.6 260.1 %copy-start.2 = (f32[1024,128]{1,0:T(8,128)S(1)}, f32[1024,128]{1,0:T(8,128)}, u32[]{:S(2)}) copy-start(f32[1024,128]{1,0:T(8,128)} %param.17) | copy-start | bytes 1572868
  32.7 10.8 %collective-permute-start.9 = (bf16[3,1,2,128,128]{4,3,2,1,0:T(8,128)(2,1)S(1)}, bf16[3,1,2,128,128]{4,3,2,1,0:T(8,128)(2,1)S(1)}, u32[]{:S(2)}, u32[]{:S(2)}) collective-permute-start(bf16[3,1,2,128,128]{4,3,2,1,0:T(8,128)(2,1)S(1)} %constant_dynamic-update-slice_fusion.3), channel_id=1, source_target_pairs={{8,0},{16,8},{24,16},{32,24},{40,32},{48,40},{56,48},{0,56},{9,1},... | collective-permute-start | bytes 589832 | tf_op jit(solution)/shard_map/ppermute | solution.py:26
  36.4 8.4 %collective-permute-start.8 = (bf16[3,1,2,128,128]{4,3,2,1,0:T(8,128)(2,1)S(1)}, bf16[3,1,2,128,128]{4,3,2,1,0:T(8,128)(2,1)S(1)}, u32[]{:S(2)}, u32[]{:S(2)}) collective-permute-start(bf16[3,1,2,128,128]{4,3,2,1,0:T(8,128)(2,1)S(1)} %constant_dynamic-update-slice_fusion.3), channel_id=1, source_target_pairs={{0,8},{8,16},{16,24},{24,32},{32,40},{40,48},{48,56},{56,0},{1,9},... | collective-permute-start | bytes 589832 | tf_op jit(solution)/shard_map/ppermute | solution.py:25
  36.4 7.1 %collective-permute-start.5 = (s32[3,3,3,1,128]{4,3,2,1,0:T(1,128)S(1)}, s32[3,3,3,1,128]{4,3,2,1,0:T(1,128)S(1)}, u32[]{:S(2)}, u32[]{:S(2)}) collective-permute-start(s32[3,3,3,1,128]{4,3,2,1,0:T(1,128)S(1)} %get-tuple-element.125), channel_id=1, source_target_pairs={{1,0},{2,1},{3,2},{4,3},{5,4},{6,5},{7,6},{0,7},{9,8},{10,9},{11,1... | collective-permute-start | bytes 41480 | tf_op jit(solution)/shard_map/ppermute | solution.py:26
  39.1 4.4 %collective-permute-start.4 = (s32[3,3,3,1,128]{4,3,2,1,0:T(1,128)S(1)}, s32[3,3,3,1,128]{4,3,2,1,0:T(1,128)S(1)}, u32[]{:S(2)}, u32[]{:S(2)}) collective-permute-start(s32[3,3,3,1,128]{4,3,2,1,0:T(1,128)S(1)} %get-tuple-element.124), channel_id=1, source_target_pairs={{0,1},{1,2},{2,3},{3,4},{4,5},{5,6},{6,7},{7,0},{8,9},{9,10},{10,1... | collective-permute-start | bytes 41480 | tf_op jit(solution)/shard_map/ppermute | solution.py:25
  44.9 256.0 %collective-permute-start.11 = (bf16[3,3,1,128,128]{4,3,2,1,0:T(8,128)(2,1)S(1)}, bf16[3,3,1,128,128]{4,3,2,1,0:T(8,128)(2,1)S(1)}, u32[]{:S(2)}, u32[]{:S(2)}) collective-permute-start(bf16[3,3,1,128,128]{4,3,2,1,0:T(8,128)(2,1)S(1)} %get-tuple-element.123), channel_id=1, source_target_pairs={{1,0},{2,1},{3,2},{4,3},{5,4},{6,5},{7,6},{0,7},{9,8},{10,9},{11,1... | collective-permute-start | bytes 884744 | tf_op jit(solution)/shard_map/ppermute | solution.py:26
  49.6 251.3 %collective-permute-start.10 = (bf16[3,3,1,128,128]{4,3,2,1,0:T(8,128)(2,1)S(1)}, bf16[3,3,1,128,128]{4,3,2,1,0:T(8,128)(2,1)S(1)}, u32[]{:S(2)}, u32[]{:S(2)}) collective-permute-start(bf16[3,3,1,128,128]{4,3,2,1,0:T(8,128)(2,1)S(1)} %get-tuple-element.122), channel_id=1, source_target_pairs={{0,1},{1,2},{2,3},{3,4},{4,5},{5,6},{6,7},{7,0},{8,9},{9,10},{10,1... | collective-permute-start | bytes 884744 | tf_op jit(solution)/shard_map/ppermute | solution.py:25
  294.3 5.2 %copy-start.4 = (f32[1024,128]{1,0:T(8,128)S(1)}, f32[1024,128]{1,0:T(8,128)}, u32[]{:S(2)}) copy-start(f32[1024,128]{1,0:T(8,128)} %get-tuple-element.119) | copy-start | bytes 1572868
  299.5 1.5 copy-start.1
  301.0 15.6 %copy-start.5 = (bf16[1024,128]{1,0:T(8,128)(2,1)S(1)}, bf16[1024,128]{1,0:T(8,128)(2,1)}, u32[]{:S(2)}) copy-start(bf16[1024,128]{1,0:T(8,128)(2,1)} %convolution_convert_fusion) | copy-start | bytes 786436
  316.6 5.4 %copy-start.7 = (bf16[256,128]{1,0:T(8,128)(2,1)S(1)}, bf16[256,128]{1,0:T(8,128)(2,1)}, u32[]{:S(2)}) copy-start(bf16[256,128]{1,0:T(8,128)(2,1)} %param.21) | copy-start | bytes 196612
  316.6 5.4 %copy-start.8 = (bf16[128,256]{1,0:T(8,128)(2,1)S(1)}, bf16[128,256]{1,0:T(8,128)(2,1)}, u32[]{:S(2)}) copy-start(bf16[128,256]{1,0:T(8,128)(2,1)} %param.20) | copy-start | bytes 196612
  316.6 5.4 %copy-start.9 = (f32[128]{0:T(128)S(1)}, f32[128]{0:T(128)}, u32[]{:S(2)}) copy-start(f32[128]{0:T(128)} %param.19) | copy-start | bytes 1540
Sparse Core Ops, SparseCore 0:
  32.7 259.8 all-reduce.2
where the time goes:
time: 331 us; the launch traced here: 330 us
  waiting for transfers between devices  245 us (74%)
  matrix products  34.8 us (11%)
  starting transfers between devices  25.2 us (8%)
  between operations  13.7 us (4%)
  other arithmetic  4.48 us (1%)
  loops' own time  4.33 us (1%)
    psum x1, waiting for transfers between devices, on_device(): lax.psum((partial_cos, partial_sin), ('gx', 'gy', 'gz'))  242 us
    ppermute x6, starting transfers between devices, extended(): after = lax.ppermute(first, axis, down)  19.2 us
  transfers between devices with their start and end apart: 13, of which 3 were waited for; matrix products, arithmetic and copies ran while one was open for 7% of the time, Pallas kernels for 0%

commit v1 on v0

v1 whole, which is shorter than its diff:
```python
import functools
import math

import jax
import jax.numpy as jnp
from jax import lax
from jax.experimental import pallas as pl
from jax.experimental.pallas import tpu as pltpu
from jax.sharding import PartitionSpec as P

MESH = pl.DeviceIdType.MESH
F32, BF16 = jnp.float32, jnp.bfloat16
NRBF = 6
GRID = 64
TILE = 128
D = 128
K = 1024
EPS = 1e-06
NX, NY, NZ = 4, 4, 8
LOG2E = 1.4426950408889634
SIN = (
    6.283182818518357,
    -41.341421396050286,
    81.5961838134782,
    -76.58009997779837,
    41.20539265997673,
    -12.271259128462068,
)
FIRST = (((0,), (0,)), ((), ()))


def rows16(values, width):
    row = lax.broadcasted_iota(jnp.int32, (16, width), 0)
    out = jnp.zeros((16, width), F32)
    for at, value in enumerate(values):
        out = jnp.where(row == at, value, out)
    return out.astype(BF16)


def sine_of_cycles(cycles):
    f = cycles - jnp.round(cycles)
    u = f * f
    acc = SIN[5]
    for c in SIN[4::-1]:
        acc = acc * u + c
    return acc * f


def lanes(tiles):
    return jnp.concatenate(tiles, axis=1)


def kernel(
    feat_hbm,
    pos_hbm,
    wave_ref,
    rmix_ref,
    cw_ref,
    filt_hbm,
    mix_ref,
    gain_ref,
    up_ref,
    down_ref,
    out_ref,
    halo,
    halo_pos,
    pair,
    pair_pos,
    tab_k,
    tab_i,
    rs_send,
    rs_recv,
    rz_send,
    rz_recv,
    filt,
    gz_send,
    gz_recv,
    ga_send,
    ga_recv,
    ls_send,
    ls_recv,
    kv,
    charge,
    q2,
    rad0,
    rad1,
    pool,
    far,
    load_sem,
    filt_sem,
    pair_sem,
    hz_sem,
    hy_sem,
    hx_sem,
    hc_sem,
    coll_sem,
):
    gx, gy, gz = lax.axis_index("gx"), lax.axis_index("gy"), lax.axis_index("gz")
    x, y, zl, zh, c = gx, gy // 2, gy % 2, gz // 2, gz % 2
    z = zh * 2 + zl
    q = x * NY + y

    def at(gx_, gy_, gz_):
        return {"gx": gx_, "gy": gy_, "gz": gz_}

    def xy_peer(i):
        return at(i // NY, (i % NY) * 2 + zl, gz)

    def z_peer(i):
        return at(gx, y * 2 + i % 2, (i // 2) * 2 + c)

    partner = at(gx, gy, gz + 1 - 2 * c)
    cross = at(gx, gy, (gz + 2 * c + 7) % 8)
    gy_up, gy_down = at(gx, (gy + 1) % 8, gz), at(gx, (gy + 7) % 8, gz)
    gx_up, gx_down = at((gx + 1) % 4, gy, gz), at((gx + 3) % 4, gy, gz)
    far_y = at(gx, (gy + 2 * zl + 7) % 8, gz)

    loads = [
        pltpu.make_async_copy(feat_hbm, halo.at[4, pl.ds(1, 2)], load_sem.at[0]),
        pltpu.make_async_copy(pos_hbm, halo_pos.at[4, pl.ds(1, 2)], load_sem.at[1]),
    ]
    for load in loads:
        load.start()
    mine = pl.multiple_of(q * 64 + z * 8, 8)
    filt_load = pltpu.make_async_copy(filt_hbm.at[pl.ds(mine, 8)], filt, filt_sem)
    filt_load.start()

    barrier = pltpu.get_barrier_semaphore()

    def greet(peer):
        pl.semaphore_signal(barrier, inc=1, device_id=peer, device_id_type=MESH)

    greet(partner)
    greet(cross)
    greet(far_y)

    def greet_xy(i, carry):
        @pl.when(i != q)
        def _():
            greet(xy_peer(i))

        return carry

    lax.fori_loop(0, NX * NY, greet_xy, 0)

    def greet_z(i, carry):
        @pl.when(i != z)
        def _():
            greet(z_peer(i))

        return carry

    lax.fori_loop(0, NZ, greet_z, 0)

    waves = wave_ref[...].astype(F32)
    kx = waves[0:1] * (4.0 / 1024.0)
    ky = waves[1:2] * (2.0 / 1024.0)
    kz = waves[2:3] * (1.0 / 1024.0)
    shift = jnp.where(c == 0, 0.25, 0.0)
    kv[...] = rows16([kx, ky, kz, kx, ky, kz], K)
    for load in loads:
        load.wait()

    def coords(pos_tile, tile_z):
        px, py, pz = (pos_tile(i).astype(F32) for i in range(3))
        return rows16(
            [
                px,
                py,
                pz,
                (gx * GRID).astype(F32),
                (gy * GRID).astype(F32),
                (tile_z * GRID).astype(F32),
            ],
            TILE,
        )

    own = [coords(lambda i, t=t: halo_pos[4, 1 + t, i], gz * 2 + t) for t in range(2)]

    def tables_k(tile_coords, first):
        def block(b, carry):
            rows = pl.ds(pl.multiple_of(b * 128, 128), 128)
            for t in range(2):
                cycles = lax.dot_general(
                    kv[:, rows], tile_coords[t], FIRST, preferred_element_type=F32
                )
                tab_k[rows, (first + t) * 128 : (first + t + 1) * 128] = sine_of_cycles(
                    cycles + shift
                ).astype(BF16)
            return carry

        lax.fori_loop(0, K // 128, block, 0)

    tables_k(own, 0)
    own_feat = halo[4, 1:3].reshape(2 * TILE, D)
    charge[0 : 2 * TILE] = jnp.dot(
        own_feat, cw_ref[...], preferred_element_type=F32
    ).astype(BF16)

    pl.semaphore_wait(barrier, 25)

    def remote(src, dst, send, recv, peer):
        return pltpu.make_async_remote_copy(
            src_ref=src,
            dst_ref=dst,
            send_sem=send,
            recv_sem=recv,
            device_id=peer,
            device_id_type=MESH,
        )

    pair_copies = [
        remote(halo.at[4, pl.ds(1, 2)], pair, pair_sem.at[0], pair_sem.at[1], partner),
        remote(
            halo_pos.at[4, pl.ds(1, 2)], pair_pos, pair_sem.at[2], pair_sem.at[3], partner
        ),
    ]
    cross_copies = [
        remote(
            halo.at[4, 1 + c], halo.at[4, 3 - 3 * c], hz_sem.at[0], hz_sem.at[1], cross
        ),
        remote(
            halo_pos.at[4, 1 + c],
            halo_pos.at[4, 3 - 3 * c],
            hz_sem.at[2],
            hz_sem.at[3],
            cross,
        ),
    ]

    def inner(col):
        return [
            remote(
                ref.at[col, 2 - c],
                ref.at[col, 3 * c],
                hc_sem.at[2 * i, col],
                hc_sem.at[2 * i + 1, col],
                partner,
            )
            for i, ref in enumerate((halo, halo_pos))
        ]

    def to_y(up):
        col, peer = (3, gy_up) if up else (5, gy_down)
        return [
            remote(
                ref.at[4, pl.ds(c, 3)],
                ref.at[col, pl.ds(c, 3)],
                hy_sem.at[2 * i, up],
                hy_sem.at[2 * i + 1, up],
                peer,
            )
            for i, ref in enumerate((halo, halo_pos))
        ]

    def to_x(up, k):
        peer = gx_up if up else gx_down
        return [
            remote(
                ref.at[3 + k, pl.ds(c, 3)],
                ref.at[(0 if up else 6) + k, pl.ds(c, 3)],
                hx_sem.at[2 * i, 3 * up + k],
                hx_sem.at[2 * i + 1, 3 * up + k],
                peer,
            )
            for i, ref in enumerate((halo, halo_pos))
        ]

    def start(copies):
        for copy in copies:
            copy.start()

    def arrived(copies):
        for copy in copies:
            copy.wait_recv()

    def sent(copies):
        for copy in copies:
            copy.wait_send()

    start(pair_copies)
    start(cross_copies)
    start(inner(4))

    arrived(pair_copies)
    other = [
        coords(lambda i, t=t: pair_pos[t, i], (gz + 1 - 2 * c) * 2 + t) for t in range(2)
    ]
    charge[2 * TILE :] = jnp.dot(
        pair[...].reshape(2 * TILE, D), cw_ref[...], preferred_element_type=F32
    ).astype(BF16)
    tables_k(other, 2)

    def rs_copy(i):
        return remote(
            rs_send.at[i], rs_recv.at[q], coll_sem.at[0], coll_sem.at[1], xy_peer(i)
        )

    def factor_block(b, carry):
        rows = pl.ds(pl.multiple_of(b * 128, 128), 128)
        part = jnp.dot(tab_k[rows, :], charge[...], preferred_element_type=F32)
        rs_send[pl.ds(b * 2, 2)] = part.astype(BF16).reshape(2, 64, D)
        for h in range(2):
            @pl.when(b * 2 + h != q)
            def _():
                rs_copy(b * 2 + h).start()

        return carry

    lax.fori_loop(0, K // 128, factor_block, 0)
    rs_recv[q] = rs_send[q]

    def all_but_one(buffer, n, sem):
        whole = buffer.at[pl.ds(0, n - 1)]
        pltpu.make_async_copy(whole, whole, sem).wait()

    arrived(cross_copies)
    start(to_y(1))
    start(to_y(0))
    start(to_x(1, 1))
    start(to_x(0, 1))

    def centre_rows(t):
        px = halo_pos[4, 1 + t, 0] - 32
        py = halo_pos[4, 1 + t, 1] - 32
        pz = halo_pos[4, 1 + t, 2] + (GRID * t - 64)
        norm = px * px + py * py + pz * pz
        high = (norm >> 8) << 8
        scale = 1.0 / 64.0
        values = [-2 * px, -2 * py, -2 * pz, high, norm - high]
        return rows16([v.astype(F32) * scale for v in values] + [scale, scale], TILE)

    targets = [centre_rows(t) for t in range(2)]

    def column(col, first):
        dx, dy = col // 3 - 1, col % 3 - 1
        px = lanes([halo_pos[col, s, 0] for s in range(4)]) + (dx * GRID - 32)
        py = lanes([halo_pos[col, s, 1] for s in range(4)]) + (dy * GRID - 32)
        pz = lanes([halo_pos[col, s, 2] + (GRID * s - 128) for s in range(4)])
        norm = px * px + py * py + pz * pz
        high = (norm >> 8) << 8
        scale = 1.0 / 64.0
        xs, ys, zs, hs, ls = (
            v.astype(F32) * scale for v in (px, py, pz, high, norm - high)
        )
        sources = rows16([xs, ys, zs, scale, scale, hs, ls], 4 * TILE)
        for t, rad in enumerate((rad0, rad1)):
            q2[t] = lax.dot_general(
                targets[t],
                sources[:, t * TILE : (t + 3) * TILE],
                FIRST,
                preferred_element_type=F32,
            )
            for part in range(8):
                rows = slice(part * 16, part * 16 + 16)
                raw = q2[t, rows]
                s2 = jnp.clip(raw, 1.0 / 8192.0, 1.0)
                s = s2 * lax.rsqrt(s2)
                rest = 1.0 - s2
                env = jnp.where(raw > 0.0, rest * rest, 0.0)
                step = jnp.exp2(s * (6.0 * LOG2E))
                value = env * jnp.exp2(s * (3.0 * LOG2E) - s2 * (18.0 * LOG2E))
                for r in range(NRBF):
                    rad[r * TILE + part * 16 : r * TILE + part * 16 + 16] = value.astype(
                        BF16
                    )
                    if r < NRBF - 1:
                        value = value * step
            near = halo[col, t : t + 3].reshape(3 * TILE, D)
            got = jnp.dot(rad[...], near, preferred_element_type=F32)
            if first:
                pool[t] = got
            else:
                pool[t] += got

    arrived(inner(4))
    column(4, True)

    everyone = lanes(own + other)
    for t in range(4):
        def block(b, carry, t=t):
            cols = pl.ds(pl.multiple_of(b * 128, 128), 128)
            cycles = lax.dot_general(
                everyone[:, t * TILE : (t + 1) * TILE],
                kv[:, cols],
                FIRST,
                preferred_element_type=F32,
            )
            tab_i[t * TILE : (t + 1) * TILE, cols] = sine_of_cycles(
                cycles + shift
            ).astype(BF16)
            return carry

        lax.fori_loop(0, K // 128, block, 0)

    for up, k in ((1, 0), (0, 2)):
        arrived(to_y(up))
        start(inner(3 + k))
        start(to_x(1, k))
        start(to_x(0, k))

    all_but_one(rs_recv, NX * NY, coll_sem.at[1])
    acc = rs_recv[0].astype(F32)
    for i in range(1, NX * NY):
        acc = acc + rs_recv[i].astype(F32)
    rz_send[...] = acc.reshape(NZ, 8, D)

    def rz_copy(i):
        return remote(rz_send.at[i], rz_recv.at[z], coll_sem.at[2], coll_sem.at[3], z_peer(i))

    def send_z(copy_of):
        def one(i, carry):
            @pl.when(i != z)
            def _():
                copy_of(i).start()

            return carry

        lax.fori_loop(0, NZ, one, 0)

    send_z(rz_copy)
    rz_recv[z] = rz_send[z]

    for k in (3, 5):
        arrived(inner(k))
        column(k, False)

    all_but_one(rz_recv, NZ, coll_sem.at[3])
    total = rz_recv[0]
    for i in range(1, NZ):
        total = total + rz_recv[i]
    filt_load.wait()
    factor = total * (1.0 / 256.0)
    filtered = jnp.dot(
        filt[...] * factor,
        mix_ref[...],
        precision=lax.Precision.HIGHEST,
        preferred_element_type=F32,
    )
    gz_send[...] = filtered

    def gz_copy(i):
        return remote(gz_send, gz_recv.at[z], coll_sem.at[4], coll_sem.at[5], z_peer(i))

    send_z(gz_copy)
    gz_recv[z] = filtered

    def relay(up):
        for k in (1, 0, 2):
            arrived(to_x(up, k))
            start(inner((0 if up else 6) + k))

    def side(up):
        for k in (1, 0, 2):
            arrived(inner((0 if up else 6) + k))
            column((0 if up else 6) + k, False)

    relay(1)
    relay(0)

    all_but_one(gz_recv, NZ, coll_sem.at[5])
    block = gz_recv[...].reshape(64, D).astype(BF16)
    ga_send[...] = block

    def ga_copy(i):
        return remote(ga_send, ga_recv.at[q], coll_sem.at[6], coll_sem.at[7], xy_peer(i))

    def send_xy(i, carry):
        @pl.when(i != q)
        def _():
            ga_copy(i).start()

        return carry

    lax.fori_loop(0, NX * NY, send_xy, 0)
    ga_recv[q] = block
    side(1)
    side(0)

    for t in range(2):
        message = jnp.zeros((TILE, D), F32)
        for r in range(NRBF):
            weight = math.exp(-18.0 * ((r + 0.5) / NRBF) ** 2)
            pooled = (pool[t, r * TILE : (r + 1) * TILE] * weight).astype(BF16)
            message = message + jnp.dot(
                pooled, rmix_ref[r * D : (r + 1) * D], preferred_element_type=F32
            )
        far[t * TILE : (t + 1) * TILE] = message + halo[4, 1 + t].astype(F32)

    all_but_one(ga_recv, NX * NY, coll_sem.at[7])
    spectrum = ga_recv[...].reshape(K, D)
    ls_send[...] = jnp.dot(
        tab_i[2 * TILE :], spectrum, preferred_element_type=F32
    )
    last = remote(ls_send, ls_recv, coll_sem.at[8], coll_sem.at[9], partner)
    last.start()
    summed = far[...] + jnp.dot(tab_i[: 2 * TILE], spectrum, preferred_element_type=F32)
    last.wait_recv()
    summed = summed + ls_recv[...]
    mean = jnp.mean(summed * summed, axis=-1, keepdims=True)
    normed = summed * lax.rsqrt(mean + EPS) * gain_ref[...]
    hidden = jnp.dot(normed.astype(BF16), up_ref[...], preferred_element_type=F32)
    hidden = hidden / (1.0 + jnp.exp(-hidden))
    updated = summed + jnp.dot(
        hidden.astype(BF16), down_ref[...], preferred_element_type=F32
    )
    out_ref[...] = updated.astype(BF16).reshape(2, TILE, D)

    sent(pair_copies)
    sent(cross_copies)
    for up in (0, 1):
        sent(to_y(up))
        for k in range(3):
            sent(to_x(up, k))
    for col in range(9):
        sent(inner(col))
    all_but_one(rs_send, NX * NY, coll_sem.at[0])
    all_but_one(rz_send, NZ, coll_sem.at[2])
    all_but_one(gz_recv, NZ, coll_sem.at[4])
    all_but_one(ga_recv, NX * NY, coll_sem.at[6])
    last.wait_send()


def on_device(features, positions, waves, rmix, cw, filters, mix, gain, up, down):
    feat = features.reshape(2, TILE, D)
    pos = positions.reshape(3, 2, 1, TILE).transpose(1, 0, 2, 3)
    vmem = pl.BlockSpec(memory_space=pltpu.VMEM)
    hbm = pl.BlockSpec(memory_space=pl.ANY)
    dma = pltpu.SemaphoreType.DMA
    out = pl.pallas_call(
        kernel,
        out_shape=jax.ShapeDtypeStruct((2, TILE, D), BF16),
        in_specs=[hbm, hbm, vmem, vmem, vmem, hbm, vmem, vmem, vmem, vmem],
        out_specs=vmem,
        scratch_shapes=[
            pltpu.VMEM((9, 4, TILE, D), BF16),
            pltpu.VMEM((9, 4, 3, 1, TILE), jnp.int32),
            pltpu.VMEM((2, TILE, D), BF16),
            pltpu.VMEM((2, 3, 1, TILE), jnp.int32),
            pltpu.VMEM((K, 4 * TILE), BF16),
            pltpu.VMEM((4 * TILE, K), BF16),
            pltpu.VMEM((16, 64, D), BF16),
            pltpu.VMEM((16, 64, D), BF16),
            pltpu.VMEM((NZ, 8, D), F32),
            pltpu.VMEM((NZ, 8, D), F32),
            pltpu.VMEM((8, D), F32),
            pltpu.VMEM((8, D), F32),
            pltpu.VMEM((NZ, 8, D), F32),
            pltpu.VMEM((64, D), BF16),
            pltpu.VMEM((16, 64, D), BF16),
            pltpu.VMEM((2 * TILE, D), F32),
            pltpu.VMEM((2 * TILE, D), F32),
            pltpu.VMEM((16, K), BF16),
            pltpu.VMEM((4 * TILE, D), BF16),
            pltpu.VMEM((2, TILE, 3 * TILE), F32),
            pltpu.VMEM((NRBF * TILE, 3 * TILE), BF16),
            pltpu.VMEM((NRBF * TILE, 3 * TILE), BF16),
            pltpu.VMEM((2, NRBF * TILE, D), F32),
            pltpu.VMEM((2 * TILE, D), F32),
            dma((2,)),
            dma,
            dma((4,)),
            dma((4,)),
            dma((4, 2)),
            dma((4, 6)),
            dma((4, 9)),
            dma((10,)),
        ],
        compiler_params=pltpu.CompilerParams(collective_id=0, has_side_effects=True),
    )(feat, pos, waves, rmix, cw, filters, mix, gain.reshape(1, D), up, down)
    return out.reshape(features.shape)


def solution(mesh):
    tiles = P("gx", "gy", "gz", None, None)
    in_specs = (tiles, P(None, "gx", "gy", "gz", None)) + (P(),) * 8
    return jax.shard_map(
        on_device, mesh=mesh, in_specs=in_specs, out_specs=tiles, check_vma=False
    )
```

time: 331 us -> 45.2 us (0.14)
  waiting for transfers between devices: 245 us -> 0 us
  Pallas kernels: 0 us -> 42.2 us
  matrix products: 34.8 us -> 0 us
  starting transfers between devices: 25.2 us -> 0 us
  between operations: 13.7 us -> 0.01 us
  other arithmetic: 4.48 us -> 0 us
  loops' own time: 4.33 us -> 0 us
    psum x1 -> x0, waiting for transfers between devices: 242 us -> none  [on_device(): lax.psum((partial_cos, partial_sin), ('gx', 'gy', 'gz'))]
    pallas_call x0 -> x1, Pallas kernels: none -> 42.2 us  [on_device(): pl.pallas_call(kernel, out_shape=jax.ShapeDtypeStruct((2, TILE, D), BF16)...]
    dot_general x12 -> x0, matrix products: 34.8 us -> none  [the longest x1 6.51 us: on_device(): jnp.dot(sin_table, charges, preferred_element_type=jnp.float32)]
    ppermute x12 -> x0, starting transfers between devices: 25.2 us -> none  [the longest x6 19.2 us: extended(): after = lax.ppermute(first, axis, down)]
    another operation x1 -> x0, loops' own time: 4.33 us -> none  [on_device(): lax.map(one_tile, jnp.arange(count_x * count_y * count_z, dtype=jnp.int32))]
  transfers between devices with their start and end apart: 13 -> 0, of which waited for: 3 -> 0; matrix products, arithmetic and copies ran while one was open for 7% -> 0% of each run, Pallas kernels for 0% -> 0%
where the time goes in v1:
time: 45.2 us; the launch traced here: 45 us
  Pallas kernels  42.2 us (93%)
  local copies, waits for them, and re-layouts  2.74 us (6%)
    pallas_call x1, Pallas kernels, on_device(): pl.pallas_call(kernel, out_shape=jax.ShapeDtypeStruct((2, TILE, D), BF16)...  42.2 us
    unnamed x3, local copies, waits for them, and re-layouts  2.16 us

profile of v1, /device:TPU:1, one launch (start us, length us, event | category | flops | bytes accessed | tf_op | source)
XLA Modules:
  0.0 45.0 jit_solution(8523392884334089471)
XLA Ops:
  0.0 0.0 copy-start
  0.0 0.7 %copy-done = s32[3,1,1,2,128]{4,3,2,1,0:T(2,128)S(1)} copy-done((s32[3,1,1,2,128]{4,3,2,1,0:T(2,128)S(1)}, s32[3,1,1,2,128]{4,3,2,1,0:T(2,128)}, u32[]{:S(2)}) %copy-start) | copy-done | bytes 3096
  0.7 0.6 %copy.14 = s32[3,2,1,128]{3,2,0,1:T(1,128)} copy(s32[3,2,1,128]{3,1,0,2:T(2,128)S(1)} %bitcast.10) | data formatting | bytes 6144 | tf_op jit(solution)/shard_map/reshape | solution.py:526
  1.3 42.2 %shard_map.100 = bf16[2,128,128]{2,1,0:T(8,128)(2,1)} custom-call(bf16[2,128,128]{2,1,0:T(8,128)(2,1)} %bitcast.8, s32[2,3,1,128]{3,2,1,0:T(1,128)} %bitcast.9, s32[3,1024]{1,0:T(4,128)} %wave_ref.1, bf16[768,128]{1,0:T(8,128)(2,1)} %rmix_ref.1, bf16[128,128]{1,0:T(8,128)(2,1)} %cw_ref.1, f32[1024,128]{1,0:T(8,128)} %filt_hbm.1, f32[128,128]{1,0:T(8,128)} %mix_ref.1, ...), custom_call_target="tpu_custom_call" | custom-call | tf_op jit(solution)/shard_map/pallas_call | solution.py:530
  43.5 1.5 %copy.16 = bf16[1,1,2,128,128]{4,3,2,1,0:T(8,128)(2,1)} copy(bf16[1,1,2,128,128]{4,3,2,1,0:T(8,128)(2,1)} %bitcast.7) | data formatting | bytes 131072
Async XLA Ops:
  0.0 0.7 %copy-start = (s32[3,1,1,2,128]{4,3,2,1,0:T(2,128)S(1)}, s32[3,1,1,2,128]{4,3,2,1,0:T(2,128)}, u32[]{:S(2)}) copy-start(s32[3,1,1,2,128]{4,3,2,1,0:T(2,128)} %param.11) | copy-start | bytes 9220

commit v2 on v1

v2 whole, which is shorter than its diff:
```python
import functools
import math

import jax
import jax.numpy as jnp
from jax import lax
from jax.experimental import pallas as pl
from jax.experimental.pallas import tpu as pltpu
from jax.sharding import PartitionSpec as P

MESH = pl.DeviceIdType.MESH
F32, BF16 = jnp.float32, jnp.bfloat16
NRBF = 6
GRID = 64
TILE = 128
D = 128
K = 1024
EPS = 1e-06
NX, NY, NZ = 4, 4, 8
LOG2E = 1.4426950408889634
ROUND = 12582912.0
SIN = (
    6.283182818518357,
    -41.341421396050286,
    81.5961838134782,
    -76.58009997779837,
    41.20539265997673,
    -12.271259128462068,
)
FIRST = (((0,), (0,)), ((), ()))


def rows16(values, width):
    row = lax.broadcasted_iota(jnp.int32, (16, width), 0)
    out = jnp.zeros((16, width), F32)
    for at, value in enumerate(values):
        out = jnp.where(row == at, value, out)
    return out


def sine_of_cycles(cycles):
    f = cycles - ((cycles + ROUND) - ROUND)
    u = f * f
    acc = SIN[5]
    for c in SIN[4::-1]:
        acc = acc * u + c
    return acc * f


def lanes(tiles):
    return jnp.concatenate(tiles, axis=1)


def kernel(
    feat_hbm,
    pos_hbm,
    wave_hbm,
    cw_hbm,
    filt_hbm,
    mix_hbm,
    rmix_hbm,
    gain_hbm,
    up_hbm,
    down_hbm,
    out_ref,
    pos_own,
    wave_ref,
    cw_ref,
    filt,
    mix_ref,
    rmix_ref,
    gain_ref,
    up_ref,
    down_ref,
    halo,
    halo_pos,
    pair_pos,
    tab_i,
    sx_send,
    sx_recv,
    s_own,
    rs_send,
    rs_recv,
    rz_send,
    rz_recv,
    ga_send,
    ga_recv,
    ls_send,
    ls_recv,
    kv,
    kt,
    ct,
    charge,
    q2,
    rad0,
    rad1,
    pool,
    far,
    load_sem,
    pair_sem,
    hz_sem,
    hy_sem,
    hx_sem,
    hc_sem,
    sx_sem,
    coll_sem,
):
    gx, gy, gz = lax.axis_index("gx"), lax.axis_index("gy"), lax.axis_index("gz")
    y, zl, zh, c = gy // 2, gy % 2, gz // 2, gz % 2
    z = zh * 2 + zl
    q = gx * NY + y

    def at(gx_, gy_, gz_):
        return {"gx": gx_, "gy": gy_, "gz": gz_}

    def xy_peer(i):
        return at(i // NY, (i % NY) * 2 + zl, gz)

    def z_peer(i):
        return at(gx, y * 2 + i % 2, (i // 2) * 2 + c)

    partner = at(gx, gy, gz + 1 - 2 * c)
    cross = at(gx, gy, (gz + 2 * c + 7) % 8)
    gy_up, gy_down = at(gx, (gy + 1) % 8, gz), at(gx, (gy + 7) % 8, gz)
    gx_up, gx_down = at((gx + 1) % 4, gy, gz), at((gx + 3) % 4, gy, gz)
    far_y = at(gx, (gy + 2 * zl + 7) % 8, gz)

    barrier = pltpu.get_barrier_semaphore()

    def greet(peer):
        pl.semaphore_signal(barrier, inc=1, device_id=peer, device_id_type=MESH)

    mine = pl.multiple_of(q * 64, 64)
    pairs = [
        (pos_hbm, pos_own),
        (wave_hbm, wave_ref),
        (feat_hbm, halo.at[4, pl.ds(1, 2)]),
        (cw_hbm, cw_ref),
        (filt_hbm.at[pl.ds(mine, 64)], filt),
        (mix_hbm, mix_ref),
        (rmix_hbm, rmix_ref),
        (gain_hbm, gain_ref),
        (up_hbm, up_ref),
        (down_hbm, down_ref),
    ]
    loads = [
        pltpu.make_async_copy(src, dst, load_sem.at[i])
        for i, (src, dst) in enumerate(pairs)
    ]
    for load in loads[:4]:
        load.start()

    greet(partner)
    greet(cross)
    greet(far_y)

    for i in range(1, NX * NY):
        greet(at((gx + i // NY) % NX, (y + i % NY) % NY * 2 + zl, gz))
    for i in range(1, NZ):
        greet(z_peer((z + i) % NZ))
    for load in loads[4:]:
        load.start()

    for load in loads[:2]:
        load.wait()
    waves = wave_ref[...].astype(F32)
    kx = waves[0:1] * (4.0 / 1024.0)
    ky = waves[1:2] * (2.0 / 1024.0)
    kz = waves[2:3] * (1.0 / 1024.0)
    waves = rows16([kx, ky, kz, kx, ky, kz, 1.0], K)
    kv[...] = waves.astype(BF16)
    kt[...] = waves.T.astype(BF16)
    quarter = jnp.where(c == 0, 0.25, 0.0)

    def coords(px, py, pz, tile_z, shift):
        offsets = [(v * GRID).astype(F32) for v in (gx, gy, tile_z)]
        return rows16(
            [px.astype(F32), py.astype(F32), pz.astype(F32)] + offsets + [shift], TILE
        )

    for t in range(2):
        for i in range(3):
            halo_pos[4, 1 + t, i] = pos_own[i, t : t + 1]

    def own_coords(shift):
        return [
            coords(*(halo_pos[4, 1 + t, i] for i in range(3)), gz * 2 + t, shift)
            for t in range(2)
        ]

    own = own_coords(quarter)
    own_half = lanes(own).astype(BF16)
    other_half = lanes(own_coords(0.25 - quarter)).astype(BF16)
    for load in loads[2:4]:
        load.wait()
    own_feat = halo[4, 1:3].reshape(2 * TILE, D)
    charge[...] = jnp.dot(own_feat, cw_ref[...], preferred_element_type=F32).astype(BF16)

    def factors(b, atoms):
        rows = pl.ds(pl.multiple_of(b * 128, 128), 128)
        cycles = jnp.dot(kt[rows], atoms, preferred_element_type=F32)
        table = sine_of_cycles(cycles).astype(BF16)
        return rows, jnp.dot(table, charge[...], preferred_element_type=F32)

    def other_block(b, carry):
        rows, part = factors(b, other_half)
        sx_send[rows] = part.astype(BF16)
        return carry

    lax.fori_loop(0, K // 128, other_block, 0, unroll=True)

    pl.semaphore_wait(barrier, 25)

    def remote(src, dst, send, recv, peer):
        return pltpu.make_async_remote_copy(
            src_ref=src,
            dst_ref=dst,
            send_sem=send,
            recv_sem=recv,
            device_id=peer,
            device_id_type=MESH,
        )

    swap = [
        remote(
            sx_send.at[pl.ds(i * 256, 256)],
            sx_recv.at[pl.ds(i * 256, 256)],
            sx_sem.at[0, i],
            sx_sem.at[1, i],
            partner,
        )
        for i in range(4)
    ]
    pair_copies = [
        remote(
            halo_pos.at[4, pl.ds(1, 2)], pair_pos, pair_sem.at[0], pair_sem.at[1], partner
        )
    ]
    cross_copies = [
        remote(
            halo.at[4, 1 + c], halo.at[4, 3 - 3 * c], hz_sem.at[0], hz_sem.at[1], cross
        ),
        remote(
            halo_pos.at[4, 1 + c],
            halo_pos.at[4, 3 - 3 * c],
            hz_sem.at[2],
            hz_sem.at[3],
            cross,
        ),
    ]

    def inner(col):
        return [
            remote(
                ref.at[col, 2 - c],
                ref.at[col, 3 * c],
                hc_sem.at[2 * i, col],
                hc_sem.at[2 * i + 1, col],
                partner,
            )
            for i, ref in enumerate((halo, halo_pos))
        ]

    def slots(ref, col, end):
        return ref.at[col, 3 * c] if end else ref.at[col, pl.ds(1, 2)]

    def to_y(up, end):
        col, peer = (3, gy_up) if up else (5, gy_down)
        return [
            remote(
                slots(ref, 4, end),
                slots(ref, col, end),
                hy_sem.at[4 * end + 2 * i, up],
                hy_sem.at[4 * end + 2 * i + 1, up],
                peer,
            )
            for i, ref in enumerate((halo, halo_pos))
        ]

    def to_x(up, k, end):
        peer = gx_up if up else gx_down
        return [
            remote(
                slots(ref, 3 + k, end),
                slots(ref, (0 if up else 6) + k, end),
                hx_sem.at[4 * end + 2 * i, 3 * up + k],
                hx_sem.at[4 * end + 2 * i + 1, 3 * up + k],
                peer,
            )
            for i, ref in enumerate((halo, halo_pos))
        ]

    def start(copies):
        for copy in copies:
            copy.start()

    def arrived(copies):
        for copy in copies:
            copy.wait_recv()

    def sent(copies):
        for copy in copies:
            copy.wait_send()

    start(cross_copies)
    start(pair_copies)
    for up in (1, 0):
        start(to_y(up, 0))
        start(to_x(up, 1, 0))
    start(swap)
    start(inner(4))

    def own_block(b, carry):
        rows, part = factors(b, own_half)
        s_own[rows] = part
        return carry

    lax.fori_loop(0, K // 128, own_block, 0, unroll=True)

    def rs_copy(i):
        return remote(
            rs_send.at[i], rs_recv.at[q], coll_sem.at[0], coll_sem.at[1], xy_peer(i)
        )

    for i in range(4):
        arrived(swap[i : i + 1])
        rows = slice(i * 256, i * 256 + 256)
        both = s_own[rows] + sx_recv[rows].astype(F32)
        rs_send[i * 4 : i * 4 + 4] = both.astype(BF16).reshape(4, 64, D)
        for h in range(4):
            @pl.when(i * 4 + h != q)
            def _():
                rs_copy(i * 4 + h).start()

    rs_recv[q] = rs_send[q]

    def all_but_one(buffer, n, sem):
        whole = buffer.at[pl.ds(0, n - 1)]
        pltpu.make_async_copy(whole, whole, sem).wait()

    def centre_rows(t):
        px = halo_pos[4, 1 + t, 0] - 32
        py = halo_pos[4, 1 + t, 1] - 32
        pz = halo_pos[4, 1 + t, 2] + (GRID * t - 64)
        norm = px * px + py * py + pz * pz
        high = (norm >> 8) << 8
        scale = 1.0 / 64.0
        values = [-2 * px, -2 * py, -2 * pz, high, norm - high]
        values = [v.astype(F32) * scale for v in values]
        return rows16(values + [scale, scale], TILE).astype(BF16)

    targets = [centre_rows(t) for t in range(2)]

    def column(col, first):
        dx, dy = col // 3 - 1, col % 3 - 1
        px = lanes([halo_pos[col, s, 0] for s in range(4)]) + (dx * GRID - 32)
        py = lanes([halo_pos[col, s, 1] for s in range(4)]) + (dy * GRID - 32)
        pz = lanes([halo_pos[col, s, 2] + (GRID * s - 128) for s in range(4)])
        norm = px * px + py * py + pz * pz
        high = (norm >> 8) << 8
        scale = 1.0 / 64.0
        xs, ys, zs, hs, ls = (
            v.astype(F32) * scale for v in (px, py, pz, high, norm - high)
        )
        sources = rows16([xs, ys, zs, scale, scale, hs, ls], 4 * TILE).astype(BF16)
        for t, rad in enumerate((rad0, rad1)):
            q2[t] = lax.dot_general(
                targets[t],
                sources[:, t * TILE : (t + 3) * TILE],
                FIRST,
                preferred_element_type=F32,
            )
            for part in range(8):
                rows = slice(part * 16, part * 16 + 16)
                raw = q2[t, rows]
                s2 = jnp.clip(raw, 1.0 / 8192.0, 1.0)
                s = s2 * lax.rsqrt(s2)
                rest = 1.0 - s2
                env = jnp.where(raw > 0.0, rest * rest, 0.0)
                step = jnp.exp2(s * (6.0 * LOG2E))
                value = env * jnp.exp2(s * (3.0 * LOG2E) - s2 * (18.0 * LOG2E))
                for r in range(NRBF):
                    rad[r * TILE + part * 16 : r * TILE + part * 16 + 16] = value.astype(
                        BF16
                    )
                    if r < NRBF - 1:
                        value = value * step
            near = halo[col, t : t + 3].reshape(3 * TILE, D)
            got = jnp.dot(rad[...], near, preferred_element_type=F32)
            if first:
                pool[t] = got
            else:
                pool[t] += got

    arrived(pair_copies)
    other = [
        coords(*(pair_pos[t, i] for i in range(3)), (gz + 1 - 2 * c) * 2 + t, quarter)
        for t in range(2)
    ]
    for t, tile in enumerate(own + other):
        ct[t * TILE : (t + 1) * TILE] = tile.T.astype(BF16)

    def table_block(b, carry):
        rows = pl.ds(pl.multiple_of(b * 64, 64), 64)
        for part in range(4):
            cols = slice(part * 256, part * 256 + 256)
            cycles = jnp.dot(ct[rows], kv[:, cols], preferred_element_type=F32)
            tab_i[rows, cols] = sine_of_cycles(cycles).astype(BF16)
        return carry

    lax.fori_loop(0, 8, table_block, 0)

    arrived(cross_copies)
    for up in (1, 0):
        start(to_y(up, 1))
        start(to_x(up, 1, 1))
    for up, k in ((1, 0), (0, 2)):
        arrived(to_y(up, 0))
        start(inner(3 + k))
        start(to_x(1, k, 0))
        start(to_x(0, k, 0))

    arrived(inner(4))
    column(4, True)

    all_but_one(rs_recv, NX * NY, coll_sem.at[1])
    acc = rs_recv[0].astype(F32)
    for i in range(1, NX * NY):
        acc = acc + rs_recv[i].astype(F32)
    rz_send[...] = acc.astype(BF16)
    rz_recv[z] = rz_send[...]

    def rz_copy(i):
        return remote(rz_send, rz_recv.at[z], coll_sem.at[2], coll_sem.at[3], z_peer(i))

    def send_z(i, carry):
        @pl.when(i != z)
        def _():
            rz_copy(i).start()

        return carry

    lax.fori_loop(0, NZ, send_z, 0)

    for up, k in ((1, 0), (0, 2)):
        arrived(to_y(up, 1))
        start(to_x(1, k, 1))
        start(to_x(0, k, 1))
    for up, col in ((1, 1), (0, 7)):
        arrived(to_x(up, 1, 0))
        start(inner(col))
    for col in (3, 5):
        arrived(inner(col))
        column(col, False)
    for up, col in ((1, 1), (0, 7)):
        arrived(to_x(up, 1, 1))
        arrived(inner(col))
        column(col, False)
    for load in loads[4:]:
        load.wait()
    mix_high = mix_ref[...].astype(BF16)
    mix_low = (mix_ref[...] - mix_high.astype(F32)).astype(BF16)

    all_but_one(rz_recv, NZ, coll_sem.at[3])
    total = rz_recv[0].astype(F32)
    for i in range(1, NZ):
        total = total + rz_recv[i].astype(F32)
    product = filt[...] * (total * (1.0 / 256.0))
    high = product.astype(BF16)
    low = (product - high.astype(F32)).astype(BF16)
    block = (
        jnp.dot(high, mix_high, preferred_element_type=F32)
        + jnp.dot(low, mix_high, preferred_element_type=F32)
        + jnp.dot(high, mix_low, preferred_element_type=F32)
    ).astype(BF16)
    ga_send[...] = block

    def ga_copy(i):
        return remote(ga_send, ga_recv.at[q], coll_sem.at[6], coll_sem.at[7], xy_peer(i))

    def send_xy(i, carry):
        @pl.when(i != q)
        def _():
            ga_copy(i).start()

        return carry

    lax.fori_loop(0, NX * NY, send_xy, 0)
    ga_recv[q] = block
    corners = ((1, 0, 0), (1, 2, 2), (0, 0, 6), (0, 2, 8))
    for up, k, col in corners:
        arrived(to_x(up, k, 0))
        start(inner(col))
    for up, k, col in corners:
        arrived(to_x(up, k, 1))
        arrived(inner(col))
        column(col, False)

    for t in range(2):
        message = jnp.zeros((TILE, D), F32)
        for r in range(NRBF):
            weight = math.exp(-18.0 * ((r + 0.5) / NRBF) ** 2)
            pooled = (pool[t, r * TILE : (r + 1) * TILE] * weight).astype(BF16)
            message = message + jnp.dot(
                pooled, rmix_ref[r * D : (r + 1) * D], preferred_element_type=F32
            )
        far[t * TILE : (t + 1) * TILE] = message + halo[4, 1 + t].astype(F32)

    all_but_one(ga_recv, NX * NY, coll_sem.at[7])
    spectrum = ga_recv[...].reshape(K, D)
    ls_send[...] = jnp.dot(
        tab_i[2 * TILE :], spectrum, preferred_element_type=F32
    )
    last = remote(ls_send, ls_recv, coll_sem.at[8], coll_sem.at[9], partner)
    last.start()
    summed = far[...] + jnp.dot(tab_i[: 2 * TILE], spectrum, preferred_element_type=F32)
    last.wait_recv()
    summed = summed + ls_recv[...]
    mean = jnp.mean(summed * summed, axis=-1, keepdims=True)
    normed = summed * lax.rsqrt(mean + EPS) * gain_ref[...]
    hidden = jnp.dot(normed.astype(BF16), up_ref[...], preferred_element_type=F32)
    hidden = hidden / (1.0 + jnp.exp(-hidden))
    updated = summed + jnp.dot(
        hidden.astype(BF16), down_ref[...], preferred_element_type=F32
    )
    out_ref[...] = updated.astype(BF16).reshape(2, TILE, D)

    sent(swap)
    sent(pair_copies)
    sent(cross_copies)
    for up in (0, 1):
        for end in (0, 1):
            sent(to_y(up, end))
            for k in range(3):
                sent(to_x(up, k, end))
    for col in range(9):
        sent(inner(col))
    all_but_one(rs_send, NX * NY, coll_sem.at[0])
    all_but_one(rz_recv, NZ, coll_sem.at[2])
    all_but_one(ga_recv, NX * NY, coll_sem.at[6])
    last.wait_send()


def on_device(features, positions, waves, rmix, cw, filters, mix, gain, up, down):
    feat = features.reshape(2, TILE, D)
    pos = positions.reshape(3, 2, TILE)
    hbm = pl.BlockSpec(memory_space=pl.ANY)
    dma = pltpu.SemaphoreType.DMA
    vmem = pltpu.VMEM
    out = pl.pallas_call(
        kernel,
        out_shape=pltpu.VMEM((2, TILE, D), BF16),
        in_specs=[hbm] * 10,
        out_specs=pl.BlockSpec(memory_space=pltpu.VMEM),
        scratch_shapes=[
            vmem((3, 2, TILE), jnp.int32),
            vmem((3, K), jnp.int32),
            vmem((D, D), BF16),
            vmem((64, D), F32),
            vmem((D, D), F32),
            vmem((NRBF * D, D), BF16),
            vmem((1, D), F32),
            vmem((D, 2 * D), BF16),
            vmem((2 * D, D), BF16),
            vmem((9, 4, TILE, D), BF16),
            vmem((9, 4, 3, 1, TILE), jnp.int32),
            vmem((2, 3, 1, TILE), jnp.int32),
            vmem((4 * TILE, K), BF16),
            vmem((K, D), BF16),
            vmem((K, D), BF16),
            vmem((K, D), F32),
            vmem((16, 64, D), BF16),
            vmem((16, 64, D), BF16),
            vmem((64, D), BF16),
            vmem((NZ, 64, D), BF16),
            vmem((64, D), BF16),
            vmem((16, 64, D), BF16),
            vmem((2 * TILE, D), F32),
            vmem((2 * TILE, D), F32),
            vmem((16, K), BF16),
            vmem((K, 16), BF16),
            vmem((4 * TILE, 16), BF16),
            vmem((2 * TILE, D), BF16),
            vmem((2, TILE, 3 * TILE), F32),
            vmem((NRBF * TILE, 3 * TILE), BF16),
            vmem((NRBF * TILE, 3 * TILE), BF16),
            vmem((2, NRBF * TILE, D), F32),
            vmem((2 * TILE, D), F32),
            dma((10,)),
            dma((2,)),
            dma((4,)),
            dma((8, 2)),
            dma((8, 6)),
            dma((4, 9)),
            dma((2, 4)),
            dma((10,)),
        ],
        compiler_params=pltpu.CompilerParams(collective_id=0, has_side_effects=True),
    )(feat, pos, waves, cw, filters, mix, rmix, gain.reshape(1, D), up, down)
    return out.reshape(features.shape)


def solution(mesh):
    tiles = P("gx", "gy", "gz", None, None)
    in_specs = (tiles, P(None, "gx", "gy", "gz", None)) + (P(),) * 8
    return jax.shard_map(
        on_device, mesh=mesh, in_specs=in_specs, out_specs=tiles, check_vma=False
    )
```

time: 45.2 us -> 33.4 us (0.74)
  Pallas kernels: 42.2 us -> 32.6 us
  local copies, waits for them, and re-layouts: 2.74 us -> 0.63 us
    pallas_call x1, Pallas kernels: 42.2 us -> 32.6 us  [on_device(): pl.pallas_call(kernel, out_shape=pltpu.VMEM((2, TILE, D), BF16), in_specs...]
    unnamed x3 -> x1, local copies, waits for them, and re-layouts: 2.16 us -> 0.63 us
    reshape x1 -> x0, local copies, waits for them, and re-layouts: 0.58 us -> none  [on_device(): pos = positions.reshape(3, 2, 1, TILE).transpose(1, 0, 2, 3)]
where the time goes in v2:
time: 33.4 us; the launch traced here: 33.3 us
  Pallas kernels  32.6 us (98%)
  local copies, waits for them, and re-layouts  0.63 us (2%)
    pallas_call x1, Pallas kernels, on_device(): pl.pallas_call(kernel, out_shape=pltpu.VMEM((2, TILE, D), BF16), in_specs...  32.6 us

profile of v2, /device:TPU:1, one launch (start us, length us, event | category | flops | bytes accessed | tf_op | source)
XLA Modules:
  0.0 33.3 jit_solution(4339551037743583277)
XLA Ops:
  0.0 32.6 %shard_map.100 = bf16[2,128,128]{2,1,0:T(8,128)(2,1)S(1)} custom-call(bf16[2,128,128]{2,1,0:T(8,128)(2,1)} %bitcast.5, s32[3,2,128]{2,1,0:T(2,128)} %bitcast.6, s32[3,1024]{1,0:T(4,128)} %wave_hbm.1, bf16[128,128]{1,0:T(8,128)(2,1)} %cw_hbm.1, f32[1024,128]{1,0:T(8,128)} %filt_hbm.1, f32[128,128]{1,0:T(8,128)} %mix_hbm.1, bf16[768,128]{1,0:T(8,128)(2,1)} %rmix_hbm.1, ...), custom_call_target="tpu_custom_call" | custom-call | tf_op jit(solution)/shard_map/pallas_call | solution.py:550
  32.6 0.6 %copy.12 = bf16[1,1,2,128,128]{4,3,2,1,0:T(8,128)(2,1)} copy(bf16[1,1,2,128,128]{4,3,2,1,0:T(8,128)(2,1)S(1)} %bitcast.4) | data formatting | bytes 131072

commit v3 on v2

v3 whole, which is shorter than its diff:
```python
import functools
import math

import jax
import jax.numpy as jnp
from jax import lax
from jax.experimental import pallas as pl
from jax.experimental.pallas import tpu as pltpu
from jax.sharding import PartitionSpec as P

MESH = pl.DeviceIdType.MESH
F32, BF16 = jnp.float32, jnp.bfloat16
NRBF = 6
GRID = 64
TILE = 128
D = 128
K = 1024
EPS = 1e-06
NX, NY, NZ = 4, 4, 8
LOG2E = 1.4426950408889634
ROUND = 12582912.0
SIN = (
    6.283182818518357,
    -41.341421396050286,
    81.5961838134782,
    -76.58009997779837,
    41.20539265997673,
    -12.271259128462068,
)
ORDER = (2, 1, 3, 0)
PLANE = [(i, j) for i in ORDER for j in ORDER if i or j]
LINE = sorted(range(1, 8), key=lambda i: -min(i, 8 - i))
FIRST = (((0,), (0,)), ((), ()))


def rows16(values, width):
    row = lax.broadcasted_iota(jnp.int32, (16, width), 0)
    out = jnp.zeros((16, width), F32)
    for at, value in enumerate(values):
        out = jnp.where(row == at, value, out)
    return out


def sine_of_cycles(cycles):
    f = cycles - ((cycles + ROUND) - ROUND)
    u = f * f
    acc = SIN[5]
    for c in SIN[4::-1]:
        acc = acc * u + c
    return acc * f


def lanes(tiles):
    return jnp.concatenate(tiles, axis=1)


def kernel(
    feat_hbm,
    pos_hbm,
    wave_hbm,
    cw_hbm,
    filt_hbm,
    mix_hbm,
    rmix_hbm,
    gain_hbm,
    up_hbm,
    down_hbm,
    out_ref,
    pos_own,
    wave_ref,
    cw_ref,
    filt,
    mix_ref,
    rmix_ref,
    gain_ref,
    up_ref,
    down_ref,
    halo,
    halo_pos,
    pair_pos,
    tab_i,
    sx_send,
    sx_recv,
    s_own,
    rs_send,
    rs_recv,
    rz_send,
    rz_recv,
    ga_send,
    ga_recv,
    ls_send,
    ls_recv,
    kv,
    kt,
    ct,
    charge,
    q2,
    rad0,
    rad1,
    pool,
    far,
    bytes_of,
    load_sem,
    send_sem,
    pair_sem,
    hz_sem,
    hy_sem,
    hx_sem,
    hc_sem,
    sx_sem,
    coll_sem,
    ga_sem,
    met_sem,
):
    gx, gy, gz = lax.axis_index("gx"), lax.axis_index("gy"), lax.axis_index("gz")
    y, zl, zh, c = gy // 2, gy % 2, gz // 2, gz % 2
    z = zh * 2 + zl
    q = gx * NY + y

    def at(gx_, gy_, gz_):
        return {"gx": gx_, "gy": gy_, "gz": gz_}

    def plane_peer(i, j):
        x_, y_ = (gx + i) % NX, (y + j) % NY
        return x_ * NY + y_, at(x_, y_ * 2 + zl, gz)

    def z_peer(i):
        return at(gx, y * 2 + i % 2, (i // 2) * 2 + c)

    partner = at(gx, gy, gz + 1 - 2 * c)
    cross = at(gx, gy, (gz + 2 * c + 7) % 8)
    gy_up, gy_down = at(gx, (gy + 1) % 8, gz), at(gx, (gy + 7) % 8, gz)
    gx_up, gx_down = at((gx + 1) % 4, gy, gz), at((gx + 3) % 4, gy, gz)
    far_y = at(gx, (gy + 2 * zl + 7) % 8, gz)

    barrier = pltpu.get_barrier_semaphore()

    def signal(sem, peer):
        pl.semaphore_signal(sem, inc=1, device_id=peer, device_id_type=MESH)

    def remote(src, dst, send, recv, peer):
        return pltpu.make_async_remote_copy(
            src_ref=src,
            dst_ref=dst,
            send_sem=send,
            recv_sem=recv,
            device_id=peer,
            device_id_type=MESH,
        )

    def all_of(ref, sem):
        pltpu.make_async_copy(ref, ref, sem).wait()

    mine = pl.multiple_of(q * 64, 64)
    pairs = [
        (pos_hbm, pos_own),
        (wave_hbm, wave_ref),
        (feat_hbm, halo.at[pl.ds(17, 2)]),
        (cw_hbm, cw_ref),
        (filt_hbm.at[pl.ds(mine, 64)], filt),
        (mix_hbm, mix_ref),
        (rmix_hbm, rmix_ref),
        (gain_hbm, gain_ref),
        (up_hbm, up_ref),
        (down_hbm, down_ref),
    ]
    loads = [
        pltpu.make_async_copy(src, dst, load_sem.at[min(i, 4)])
        for i, (src, dst) in enumerate(pairs)
    ]
    for load in loads[:4]:
        load.start()

    for load in loads[4:]:
        load.start()

    @pl.when(c == 1)
    def _():
        signal(barrier, partner)
        pl.semaphore_wait(met_sem, 1)
        for i, j in PLANE:
            signal(barrier, plane_peer(i, j)[1])
        for i in LINE:
            signal(barrier, z_peer((z + i) % NZ))
        signal(barrier, far_y)

    @pl.when(c == 0)
    def _():
        pl.semaphore_wait(barrier, 1)
        signal(met_sem, partner)

    for load in loads[:2]:
        load.wait()
    waves = wave_ref[...].astype(F32)
    kx = waves[0:1] * (4.0 / 1024.0)
    ky = waves[1:2] * (2.0 / 1024.0)
    kz = waves[2:3] * (1.0 / 1024.0)
    waves = rows16([kx, ky, kz, kx, ky, kz, 1.0], K)
    kv[...] = waves
    kt[...] = waves.T.astype(BF16)
    quarter = jnp.where(c == 0, 0.25, 0.0)

    def coords(px, py, pz, tile_z, shift):
        offsets = [(v * GRID).astype(F32) for v in (gx, gy, tile_z)]
        return rows16(
            [px.astype(F32), py.astype(F32), pz.astype(F32)] + offsets + [shift], TILE
        )

    for t in range(2):
        for i in range(3):
            halo_pos[17 + t, i] = pos_own[i, t : t + 1]

    def own_coords(shift):
        return [
            coords(*(halo_pos[17 + t, i] for i in range(3)), gz * 2 + t, shift)
            for t in range(2)
        ]

    own = own_coords(quarter)
    own_half = lanes(own).astype(BF16)
    other_half = lanes(own_coords(0.25 - quarter)).astype(BF16)
    for load in loads[2:4]:
        load.wait()
    own_feat = halo[17:19].reshape(2 * TILE, D)
    charge[...] = jnp.dot(own_feat, cw_ref[...], preferred_element_type=F32).astype(BF16)

    def factors(b, atoms):
        rows = pl.ds(pl.multiple_of(b * 128, 128), 128)
        cycles = jnp.dot(kt[rows], atoms, preferred_element_type=F32)
        table = sine_of_cycles(cycles).astype(BF16)
        return rows, jnp.dot(table, charge[...], preferred_element_type=F32)

    def group(i):
        return pl.multiple_of((gx + i) % NX * 256, 256)

    for i in ORDER:
        for h in range(2):
            rows, part = factors(group(i) // 128 + h, other_half)
            sx_send[rows] = part.astype(BF16)
        rows = pl.ds(group(i), 256)
        remote(
            sx_send.at[rows], sx_recv.at[rows], send_sem.at[2], sx_sem.at[i], partner
        ).start()

    for i in ORDER:
        for h in range(2):
            rows, part = factors(group(i) // 128 + h, own_half)
            s_own[rows] = part

    for i in ORDER:
        rows = pl.ds(group(i), 256)
        all_of(sx_recv.at[rows], sx_sem.at[i])
        both = s_own[rows] + sx_recv[rows].astype(F32)
        rs_send[pl.ds(group(i) // 64, 4)] = both.astype(BF16).reshape(4, 64, D)

    @pl.when(c == 1)
    def _():
        pl.semaphore_wait(barrier, 23)
        signal(met_sem, partner)

    @pl.when(c == 0)
    def _():
        pl.semaphore_wait(met_sem, 1)

    for i, j in PLANE:
        block, peer = plane_peer(i, j)
        remote(
            rs_send.at[block], rs_recv.at[q], coll_sem.at[0], coll_sem.at[1], peer
        ).start()

    def tiles(src, dst, n, sem, peer):
        return [
            remote(
                ref.at[pl.ds(src, n)], ref.at[pl.ds(dst, n)], send_sem.at[i], sem, peer
            )
            for i, ref in enumerate((halo, halo_pos))
        ]

    def got_tiles(n, sem):
        all_of(bytes_of.at[pl.ds(0, 67 * n)], sem)

    pair_copy = remote(
        halo_pos.at[pl.ds(17, 2)], pair_pos, send_sem.at[1], pair_sem, partner
    )

    def inner(col):
        return tiles(col * 4 + 2 - c, col * 4 + 3 * c, 1, hc_sem.at[col], partner)

    def sides(src, dst, end, sem, peer):
        if end:
            return tiles(src * 4 + 3 * c, dst * 4 + 3 * c, 1, sem, peer)
        return tiles(src * 4 + 1, dst * 4 + 1, 2, sem, peer)

    def to_y(up, end):
        col, peer = (3, gy_up) if up else (5, gy_down)
        return sides(4, col, end, hy_sem.at[end, up], peer)

    def to_x(up, k, end):
        peer = gx_up if up else gx_down
        dst = (0 if up else 6) + k
        return sides(3 + k, dst, end, hx_sem.at[end, 3 * up + k], peer)

    def start(copies):
        for copy in copies:
            copy.start()

    def got_y(up, end):
        got_tiles(2 - end, hy_sem.at[end, up])

    def got_x(up, k, end):
        got_tiles(2 - end, hx_sem.at[end, 3 * up + k])

    def got_inner(col):
        got_tiles(1, hc_sem.at[col])

    start(tiles(17 + c, 19 - 3 * c, 1, hz_sem, cross))
    pair_copy.start()
    for up in (1, 0):
        start(to_y(up, 0))
        start(to_x(up, 1, 0))
    start(inner(4))
    rs_recv[q] = rs_send[q]

    def all_but_one(buffer, n, sem):
        all_of(buffer.at[pl.ds(0, n - 1)], sem)

    def centre_rows(t):
        px = halo_pos[17 + t, 0] - 32
        py = halo_pos[17 + t, 1] - 32
        pz = halo_pos[17 + t, 2] + (GRID * t - 64)
        norm = px * px + py * py + pz * pz
        high = (norm >> 8) << 8
        scale = 1.0 / 64.0
        values = [-2 * px, -2 * py, -2 * pz, high, norm - high]
        values = [v.astype(F32) * scale for v in values]
        return rows16(values + [scale, scale], TILE).astype(BF16)

    targets = [centre_rows(t) for t in range(2)]

    def column(col, first):
        dx, dy = col // 3 - 1, col % 3 - 1
        px = lanes([halo_pos[col * 4 + s, 0] for s in range(4)]) + (dx * GRID - 32)
        py = lanes([halo_pos[col * 4 + s, 1] for s in range(4)]) + (dy * GRID - 32)
        pz = lanes([halo_pos[col * 4 + s, 2] + (GRID * s - 128) for s in range(4)])
        norm = px * px + py * py + pz * pz
        high = (norm >> 8) << 8
        scale = 1.0 / 64.0
        xs, ys, zs, hs, ls = (
            v.astype(F32) * scale for v in (px, py, pz, high, norm - high)
        )
        sources = rows16([xs, ys, zs, scale, scale, hs, ls], 4 * TILE).astype(BF16)
        for t, rad in enumerate((rad0, rad1)):
            q2[t] = lax.dot_general(
                targets[t],
                sources[:, t * TILE : (t + 3) * TILE],
                FIRST,
                preferred_element_type=F32,
            )
            for part in range(8):
                rows = slice(part * 16, part * 16 + 16)
                raw = q2[t, rows]
                s2 = jnp.clip(raw, 1.0 / 8192.0, 1.0)
                s = s2 * lax.rsqrt(s2)
                rest = 1.0 - s2
                env = jnp.where(raw > 0.0, rest * rest, 0.0)
                step = jnp.exp2(s * (6.0 * LOG2E))
                value = env * jnp.exp2(s * (3.0 * LOG2E) - s2 * (18.0 * LOG2E))
                for r in range(NRBF):
                    rad[r * TILE + part * 16 : r * TILE + part * 16 + 16] = value.astype(
                        BF16
                    )
                    if r < NRBF - 1:
                        value = value * step
            near = halo[col * 4 + t : col * 4 + t + 3].reshape(3 * TILE, D)
            got = jnp.dot(rad[...], near, preferred_element_type=F32)
            if first:
                pool[t] = got
            else:
                pool[t] += got

    pair_copy.wait_recv()
    other = [
        coords(*(pair_pos[t, i] for i in range(3)), (gz + 1 - 2 * c) * 2 + t, quarter)
        for t in range(2)
    ]
    for t, tile in enumerate(own + other):
        ct[t * TILE : (t + 1) * TILE] = tile.T.astype(BF16)

    turned = []
    for i in range(4):
        part = kv[:, pl.ds(group(i), 256)]
        turned.append(pltpu.roll(part, (NY - y) % NY * 64, axis=1).astype(BF16))

    def table_block(b, carry):
        rows = pl.ds(pl.multiple_of(b * 64, 64), 64)
        for part in range(4):
            cols = slice(part * 256, part * 256 + 256)
            cycles = jnp.dot(ct[rows], turned[part], preferred_element_type=F32)
            tab_i[rows, cols] = sine_of_cycles(cycles).astype(BF16)
        return carry

    lax.fori_loop(0, 8, table_block, 0)

    got_tiles(1, hz_sem)
    for up in (1, 0):
        start(to_y(up, 1))
        start(to_x(up, 1, 1))

    got_inner(4)
    column(4, True)

    all_but_one(rs_recv, NX * NY, coll_sem.at[1])
    acc = rs_recv[0].astype(F32)
    for i in range(1, NX * NY):
        acc = acc + rs_recv[i].astype(F32)
    rz_send[...] = acc.astype(BF16)
    rz_recv[z] = rz_send[...]

    for i in LINE:
        remote(
            rz_send,
            rz_recv.at[z],
            coll_sem.at[2],
            coll_sem.at[3],
            z_peer((z + i) % NZ),
        ).start()

    for up, k in ((1, 0), (0, 2)):
        got_y(up, 0)
        start(inner(3 + k))
        start(to_x(1, k, 0))
        start(to_x(0, k, 0))
    for up, col in ((1, 1), (0, 7)):
        got_x(up, 1, 0)
        start(inner(col))
    for up, k in ((1, 0), (0, 2)):
        got_y(up, 1)
        start(to_x(1, k, 1))
        start(to_x(0, k, 1))
    for col in (3, 5):
        got_inner(col)
        column(col, False)
    for up, col in ((1, 1), (0, 7)):
        got_x(up, 1, 1)
        got_inner(col)
        column(col, False)
    all_of(bytes_of, load_sem.at[4])
    mix_high = mix_ref[...].astype(BF16)
    mix_low = (mix_ref[...] - mix_high.astype(F32)).astype(BF16)

    all_but_one(rz_recv, NZ, coll_sem.at[3])
    total = rz_recv[0].astype(F32)
    for i in range(1, NZ):
        total = total + rz_recv[i].astype(F32)
    product = filt[...] * (total * (1.0 / 256.0))
    high = product.astype(BF16)
    low = (product - high.astype(F32)).astype(BF16)
    block = (
        jnp.dot(high, mix_high, preferred_element_type=F32)
        + jnp.dot(low, mix_high, preferred_element_type=F32)
        + jnp.dot(high, mix_low, preferred_element_type=F32)
    ).astype(BF16)
    ga_send[...] = block

    for i, j in PLANE:
        back = (4 - i) % 4
        remote(
            ga_send,
            ga_recv.at[back * 4 + (4 - j) % 4],
            coll_sem.at[4],
            ga_sem.at[back],
            plane_peer(i, j)[1],
        ).start()
    ga_recv[0] = block
    corners = ((1, 0, 0), (1, 2, 2), (0, 0, 6), (0, 2, 8))
    for up, k, col in corners:
        got_x(up, k, 0)
        start(inner(col))
    for up, k, col in corners:
        got_x(up, k, 1)
        got_inner(col)
        column(col, False)

    for t in range(2):
        message = jnp.zeros((TILE, D), F32)
        for r in range(NRBF):
            weight = math.exp(-18.0 * ((r + 0.5) / NRBF) ** 2)
            pooled = (pool[t, r * TILE : (r + 1) * TILE] * weight).astype(BF16)
            message = message + jnp.dot(
                pooled, rmix_ref[r * D : (r + 1) * D], preferred_element_type=F32
            )
        far[t * TILE : (t + 1) * TILE] = message + halo[17 + t].astype(F32)

    theirs, ours = 0.0, far[...]
    for i in (0, 1, 3, 2):
        some = ga_recv.at[pl.ds(i * 4, 4 if i else 3)]
        all_of(some, ga_sem.at[i])
        cols = slice(i * 256, i * 256 + 256)
        spectrum = ga_recv[i * 4 : i * 4 + 4].reshape(256, D)
        theirs = theirs + jnp.dot(
            tab_i[2 * TILE :, cols], spectrum, preferred_element_type=F32
        )
        if i == 2:
            ls_send[...] = theirs
            last = remote(ls_send, ls_recv, coll_sem.at[5], coll_sem.at[6], partner)
            last.start()
        ours = ours + jnp.dot(
            tab_i[: 2 * TILE, cols], spectrum, preferred_element_type=F32
        )
    last.wait_recv()
    summed = ours + ls_recv[...]
    mean = jnp.mean(summed * summed, axis=-1, keepdims=True)
    normed = summed * lax.rsqrt(mean + EPS) * gain_ref[...]
    hidden = jnp.dot(normed.astype(BF16), up_ref[...], preferred_element_type=F32)
    hidden = hidden / (1.0 + jnp.exp(-hidden))
    updated = summed + jnp.dot(
        hidden.astype(BF16), down_ref[...], preferred_element_type=F32
    )
    out_ref[...] = updated.astype(BF16).reshape(2, TILE, D)

    all_of(halo.at[pl.ds(0, 34)], send_sem.at[0])
    all_of(halo_pos, send_sem.at[1])
    all_of(sx_send, send_sem.at[2])
    all_but_one(rs_send, NX * NY, coll_sem.at[0])
    all_but_one(rz_recv, NZ, coll_sem.at[2])
    all_but_one(ga_recv, NX * NY, coll_sem.at[4])
    all_of(ls_send, coll_sem.at[5])


def on_device(features, positions, waves, rmix, cw, filters, mix, gain, up, down):
    feat = features.reshape(2, TILE, D)
    pos = positions.reshape(3, 2, TILE)
    hbm = pl.BlockSpec(memory_space=pl.ANY)
    dma = pltpu.SemaphoreType.DMA
    vmem = pltpu.VMEM
    out = pl.pallas_call(
        kernel,
        out_shape=pltpu.VMEM((2, TILE, D), BF16),
        in_specs=[hbm] * 10,
        out_specs=pl.BlockSpec(memory_space=pltpu.VMEM),
        scratch_shapes=[
            vmem((3, 2, TILE), jnp.int32),
            vmem((3, K), jnp.int32),
            vmem((D, D), BF16),
            vmem((64, D), F32),
            vmem((D, D), F32),
            vmem((NRBF * D, D), BF16),
            vmem((1, D), F32),
            vmem((D, 2 * D), BF16),
            vmem((2 * D, D), BF16),
            vmem((36, TILE, D), BF16),
            vmem((36, 3, 1, TILE), jnp.int32),
            vmem((2, 3, 1, TILE), jnp.int32),
            vmem((4 * TILE, K), BF16),
            vmem((K, D), BF16),
            vmem((K, D), BF16),
            vmem((K, D), F32),
            vmem((16, 64, D), BF16),
            vmem((16, 64, D), BF16),
            vmem((64, D), BF16),
            vmem((NZ, 64, D), BF16),
            vmem((64, D), BF16),
            vmem((16, 64, D), BF16),
            vmem((2 * TILE, D), F32),
            vmem((2 * TILE, D), F32),
            vmem((16, K), F32),
            vmem((K, 16), BF16),
            vmem((4 * TILE, 16), BF16),
            vmem((2 * TILE, D), BF16),
            vmem((2, TILE, 3 * TILE), F32),
            vmem((NRBF * TILE, 3 * TILE), BF16),
            vmem((NRBF * TILE, 3 * TILE), BF16),
            vmem((2, NRBF * TILE, D), F32),
            vmem((2 * TILE, D), F32),
            vmem((833, 1, D), F32),
            dma((5,)),
            dma((3,)),
            dma,
            dma,
            dma((2, 2)),
            dma((2, 6)),
            dma((9,)),
            dma((4,)),
            dma((7,)),
            dma((4,)),
            pltpu.SemaphoreType.REGULAR,
        ],
        compiler_params=pltpu.CompilerParams(collective_id=0, has_side_effects=True),
    )(feat, pos, waves, cw, filters, mix, rmix, gain.reshape(1, D), up, down)
    return out.reshape(features.shape)


def solution(mesh):
    tiles = P("gx", "gy", "gz", None, None)
    in_specs = (tiles, P(None, "gx", "gy", "gz", None)) + (P(),) * 8
    return jax.shard_map(
        on_device, mesh=mesh, in_specs=in_specs, out_specs=tiles, check_vma=False
    )
```

time: 33.4 us -> 31.9 us (0.955)
  Pallas kernels: 32.6 us -> 31.2 us
    pallas_call x1, Pallas kernels: 32.6 us -> 31.2 us  [on_device(): pl.pallas_call(kernel, out_shape=pltpu.VMEM((2, TILE, D), BF16), in_specs...]
where the time goes in v3:
time: 31.9 us; the launch traced here: 31.8 us
  Pallas kernels  31.2 us (98%)
  local copies, waits for them, and re-layouts  0.63 us (2%)
    pallas_call x1, Pallas kernels, on_device(): pl.pallas_call(kernel, out_shape=pltpu.VMEM((2, TILE, D), BF16), in_specs...  31.2 us

profile of v3, /device:TPU:1, one launch (start us, length us, event | category | flops | bytes accessed | tf_op | source)
XLA Modules:
  0.0 31.8 jit_solution(4679493809202597466)
XLA Ops:
  0.0 31.2 %shard_map.100 = bf16[2,128,128]{2,1,0:T(8,128)(2,1)S(1)} custom-call(bf16[2,128,128]{2,1,0:T(8,128)(2,1)} %bitcast.5, s32[3,2,128]{2,1,0:T(2,128)} %bitcast.6, s32[3,1024]{1,0:T(4,128)} %wave_hbm.1, bf16[128,128]{1,0:T(8,128)(2,1)} %cw_hbm.1, f32[1024,128]{1,0:T(8,128)} %filt_hbm.1, f32[128,128]{1,0:T(8,128)} %mix_hbm.1, bf16[768,128]{1,0:T(8,128)(2,1)} %rmix_hbm.1, ...), custom_call_target="tpu_custom_call" | custom-call | tf_op jit(solution)/shard_map/pallas_call | solution.py:536
  31.2 0.6 %copy.12 = bf16[1,1,2,128,128]{4,3,2,1,0:T(8,128)(2,1)} copy(bf16[1,1,2,128,128]{4,3,2,1,0:T(8,128)(2,1)S(1)} %bitcast.4) | data formatting | bytes 131072

commit v4 on v3

--- a/solution.py
+++ b/solution.py
@@ -95,8 +95,11 @@
     ct,
     charge,
     q2,
+    targets,
     rad0,
     rad1,
+    rad2,
+    rad3,
     pool,
     far,
     bytes_of,
@@ -237,6 +240,7 @@
         for h in range(2):
             rows, part = factors(group(i) // 128 + h, other_half)
             sx_send[rows] = part.astype(BF16)
+    for i in ORDER:
         rows = pl.ds(group(i), 256)
         remote(
             sx_send.at[rows], sx_recv.at[rows], send_sem.at[2], sx_sem.at[i], partner
@@ -333,50 +337,74 @@
         scale = 1.0 / 64.0
         values = [-2 * px, -2 * py, -2 * pz, high, norm - high]
         values = [v.astype(F32) * scale for v in values]
-        return rows16(values + [scale, scale], TILE).astype(BF16)
-
-    targets = [centre_rows(t) for t in range(2)]
-
-    def column(col, first):
-        dx, dy = col // 3 - 1, col % 3 - 1
-        px = lanes([halo_pos[col * 4 + s, 0] for s in range(4)]) + (dx * GRID - 32)
-        py = lanes([halo_pos[col * 4 + s, 1] for s in range(4)]) + (dy * GRID - 32)
-        pz = lanes([halo_pos[col * 4 + s, 2] + (GRID * s - 128) for s in range(4)])
-        norm = px * px + py * py + pz * pz
-        high = (norm >> 8) << 8
-        scale = 1.0 / 64.0
-        xs, ys, zs, hs, ls = (
-            v.astype(F32) * scale for v in (px, py, pz, high, norm - high)
-        )
-        sources = rows16([xs, ys, zs, scale, scale, hs, ls], 4 * TILE).astype(BF16)
-        for t, rad in enumerate((rad0, rad1)):
-            q2[t] = lax.dot_general(
-                targets[t],
-                sources[:, t * TILE : (t + 3) * TILE],
-                FIRST,
-                preferred_element_type=F32,
+        return rows16(values + [scale, scale], TILE)
+
+    for t in range(2):
+        targets[t] = centre_rows(t).T.astype(BF16)
+
+    def radial_steps(col, slot):
+        def squares():
+            dx, dy = col // 3 - 1, col % 3 - 1
+            at_ = [[halo_pos[col * 4 + s, i] for s in range(4)] for i in range(3)]
+            px = lanes(at_[0]) + (dx * GRID - 32)
+            py = lanes(at_[1]) + (dy * GRID - 32)
+            pz = lanes([at_[2][s] + (GRID * s - 128) for s in range(4)])
+            norm = px * px + py * py + pz * pz
+            high = (norm >> 8) << 8
+            scale = 1.0 / 64.0
+            xs, ys, zs, hs, ls = (
+                v.astype(F32) * scale for v in (px, py, pz, high, norm - high)
             )
-            for part in range(8):
-                rows = slice(part * 16, part * 16 + 16)
-                raw = q2[t, rows]
-                s2 = jnp.clip(raw, 1.0 / 8192.0, 1.0)
-                s = s2 * lax.rsqrt(s2)
-                rest = 1.0 - s2
-                env = jnp.where(raw > 0.0, rest * rest, 0.0)
-                step = jnp.exp2(s * (6.0 * LOG2E))
-                value = env * jnp.exp2(s * (3.0 * LOG2E) - s2 * (18.0 * LOG2E))
-                for r in range(NRBF):
-                    rad[r * TILE + part * 16 : r * TILE + part * 16 + 16] = value.astype(
-                        BF16
-                    )
-                    if r < NRBF - 1:
-                        value = value * step
+            sources = rows16(
+                [xs, ys, zs, scale, scale, hs, ls], 4 * TILE
+            ).astype(BF16)
+            for t in range(2):
+                q2[slot, t] = jnp.dot(
+                    targets[t],
+                    sources[:, t * TILE : (t + 3) * TILE],
+                    preferred_element_type=F32,
+                )
+
+        def some(t, part):
+            rad = rads[slot * 2 + t]
+            raw = q2[slot, t, part * 16 : part * 16 + 16]
+            s2 = jnp.clip(raw, 1.0 / 8192.0, 1.0)
+            s = s2 * lax.rsqrt(s2)
+            rest = 1.0 - s2
+            env = jnp.where(raw > 0.0, rest * rest, 0.0)
+            step = jnp.exp2(s * (6.0 * LOG2E))
+            value = env * jnp.exp2(s * (3.0 * LOG2E) - s2 * (18.0 * LOG2E))
+            for r in range(NRBF):
+                first = r * TILE + part * 16
+                rad[first : first + 16] = value.astype(BF16)
+                if r < NRBF - 1:
+                    value = value * step
+
+        return [squares] + [
+            functools.partial(some, t, part) for t in range(2) for part in range(8)
+        ]
+
+    def pool_steps(col, slot, first=False):
+        def some(t, r):
             near = halo[col * 4 + t : col * 4 + t + 3].reshape(3 * TILE, D)
-            got = jnp.dot(rad[...], near, preferred_element_type=F32)
+            rows = slice(r * TILE, r * TILE + TILE)
+            got = jnp.dot(rads[slot * 2 + t][rows], near, preferred_element_type=F32)
             if first:
-                pool[t] = got
+                pool[t, rows] = got
             else:
-                pool[t] += got
+                pool[t, rows] += got
+
+        return [functools.partial(some, t, r) for t in range(2) for r in range(NRBF)]
+
+    def weave(one, two):
+        done = 0
+        for i, step in enumerate(one):
+            step()
+            while done * len(one) < (i + 1) * len(two):
+                two[done]()
+                done += 1
+
+    rads = (rad0, rad1, rad2, rad3)
 
     pair_copy.wait_recv()
     other = [
@@ -407,7 +435,8 @@
         start(to_x(up, 1, 1))
 
     got_inner(4)
-    column(4, True)
+    weave(radial_steps(4, 0), [])
+    weave(pool_steps(4, 0, True), [])
 
     all_but_one(rs_recv, NX * NY, coll_sem.at[1])
     acc = rs_recv[0].astype(F32)
@@ -437,13 +466,16 @@
         got_y(up, 1)
         start(to_x(1, k, 1))
         start(to_x(0, k, 1))
-    for col in (3, 5):
-        got_inner(col)
-        column(col, False)
-    for up, col in ((1, 1), (0, 7)):
-        got_x(up, 1, 1)
-        got_inner(col)
-        column(col, False)
+    got_inner(3)
+    weave(radial_steps(3, 0), [])
+    got_inner(5)
+    weave(radial_steps(5, 1), pool_steps(3, 0))
+    got_x(1, 1, 1)
+    got_inner(1)
+    weave(radial_steps(1, 0), pool_steps(5, 1))
+    got_x(0, 1, 1)
+    got_inner(7)
+    weave(radial_steps(7, 1), pool_steps(1, 0))
     all_of(bytes_of, load_sem.at[4])
     mix_high = mix_ref[...].astype(BF16)
     mix_low = (mix_ref[...] - mix_high.astype(F32)).astype(BF16)
@@ -476,10 +508,13 @@
     for up, k, col in corners:
         got_x(up, k, 0)
         start(inner(col))
-    for up, k, col in corners:
+    before = pool_steps(7, 1)
+    for i, (up, k, col) in enumerate(corners):
         got_x(up, k, 1)
         got_inner(col)
-        column(col, False)
+        weave(radial_steps(col, i % 2), before)
+        before = pool_steps(col, i % 2)
+    weave(before, [])
 
     for t in range(2):
         message = jnp.zeros((TILE, D), F32)
@@ -491,7 +526,7 @@
             )
         far[t * TILE : (t + 1) * TILE] = message + halo[17 + t].astype(F32)
 
-    theirs, ours = 0.0, far[...]
+    theirs = 0.0
     for i in (0, 1, 3, 2):
         some = ga_recv.at[pl.ds(i * 4, 4 if i else 3)]
         all_of(some, ga_sem.at[i])
@@ -500,13 +535,12 @@
         theirs = theirs + jnp.dot(
             tab_i[2 * TILE :, cols], spectrum, preferred_element_type=F32
         )
-        if i == 2:
-            ls_send[...] = theirs
-            last = remote(ls_send, ls_recv, coll_sem.at[5], coll_sem.at[6], partner)
-            last.start()
-        ours = ours + jnp.dot(
-            tab_i[: 2 * TILE, cols], spectrum, preferred_element_type=F32
-        )
+    ls_send[...] = theirs
+    last = remote(ls_send, ls_recv, coll_sem.at[5], coll_sem.at[6], partner)
+    last.start()
+    ours = far[...] + jnp.dot(
+        tab_i[: 2 * TILE], ga_recv[...].reshape(K, D), preferred_element_type=F32
+    )
     last.wait_recv()
     summed = ours + ls_recv[...]
     mean = jnp.mean(summed * summed, axis=-1, keepdims=True)
@@ -567,7 +601,10 @@
             vmem((K, 16), BF16),
             vmem((4 * TILE, 16), BF16),
             vmem((2 * TILE, D), BF16),
-            vmem((2, TILE, 3 * TILE), F32),
+            vmem((2, 2, TILE, 3 * TILE), F32),
+            vmem((2, TILE, 16), BF16),
+            vmem((NRBF * TILE, 3 * TILE), BF16),
+            vmem((NRBF * TILE, 3 * TILE), BF16),
             vmem((NRBF * TILE, 3 * TILE), BF16),
             vmem((NRBF * TILE, 3 * TILE), BF16),
             vmem((2, NRBF * TILE, D), F32),

time: 31.9 us -> 31.6 us (level)
  Pallas kernels: 31.2 us -> 30.8 us
    pallas_call x1, Pallas kernels: 31.2 us -> 30.8 us  [on_device(): pl.pallas_call(kernel, out_shape=pltpu.VMEM((2, TILE, D), BF16), in_specs...]
where the time goes in v4:
time: 31.6 us; the launch traced here: 31.5 us
  Pallas kernels  30.8 us (97%)
  local copies, waits for them, and re-layouts  0.63 us (2%)
    pallas_call x1, Pallas kernels, on_device(): pl.pallas_call(kernel, out_shape=pltpu.VMEM((2, TILE, D), BF16), in_specs...  30.8 us
    unnamed x1, local copies, waits for them, and re-layouts  0.63 us

profile of v4, /device:TPU:1, one launch (start us, length us, event | category | flops | bytes accessed | tf_op | source)
XLA Modules:
  0.0 31.5 jit_solution(14622812008886190503)
XLA Ops:
  0.0 30.8 %shard_map.100 = bf16[2,128,128]{2,1,0:T(8,128)(2,1)S(1)} custom-call(bf16[2,128,128]{2,1,0:T(8,128)(2,1)} %bitcast.5, s32[3,2,128]{2,1,0:T(2,128)} %bitcast.6, s32[3,1024]{1,0:T(4,128)} %wave_hbm.1, bf16[128,128]{1,0:T(8,128)(2,1)} %cw_hbm.1, f32[1024,128]{1,0:T(8,128)} %filt_hbm.1, f32[128,128]{1,0:T(8,128)} %mix_hbm.1, bf16[768,128]{1,0:T(8,128)(2,1)} %rmix_hbm.1, ...), custom_call_target="tpu_custom_call" | custom-call | tf_op jit(solution)/shard_map/pallas_call | solution.py:570
  30.8 0.6 %copy.12 = bf16[1,1,2,128,128]{4,3,2,1,0:T(8,128)(2,1)} copy(bf16[1,1,2,128,128]{4,3,2,1,0:T(8,128)(2,1)S(1)} %bitcast.4) | data formatting | bytes 131072

commit v5 on v4

--- a/solution.py
+++ b/solution.py
@@ -29,6 +29,7 @@
 )
 ORDER = (2, 1, 3, 0)
 PLANE = [(i, j) for i in ORDER for j in ORDER if i or j]
+INNER = (3, 2, 4, 1, 0, 1, 5, 2, 6)
 LINE = sorted(range(1, 8), key=lambda i: -min(i, 8 - i))
 FIRST = (((0,), (0,)), ((), ()))
 
@@ -243,7 +244,7 @@
     for i in ORDER:
         rows = pl.ds(group(i), 256)
         remote(
-            sx_send.at[rows], sx_recv.at[rows], send_sem.at[2], sx_sem.at[i], partner
+            sx_send.at[rows], sx_recv.at[rows], send_sem.at[2], sx_sem, partner
         ).start()
 
     for i in ORDER:
@@ -251,9 +252,9 @@
             rows, part = factors(group(i) // 128 + h, own_half)
             s_own[rows] = part
 
+    all_of(sx_recv, sx_sem)
     for i in ORDER:
         rows = pl.ds(group(i), 256)
-        all_of(sx_recv.at[rows], sx_sem.at[i])
         both = s_own[rows] + sx_recv[rows].astype(F32)
         rs_send[pl.ds(group(i) // 64, 4)] = both.astype(BF16).reshape(4, 64, D)
 
@@ -288,7 +289,7 @@
     )
 
     def inner(col):
-        return tiles(col * 4 + 2 - c, col * 4 + 3 * c, 1, hc_sem.at[col], partner)
+        return tiles(col * 4 + 2 - c, col * 4 + 3 * c, 1, hc_sem.at[INNER[col]], partner)
 
     def sides(src, dst, end, sem, peer):
         if end:
@@ -297,30 +298,41 @@
 
     def to_y(up, end):
         col, peer = (3, gy_up) if up else (5, gy_down)
-        return sides(4, col, end, hy_sem.at[end, up], peer)
+        return sides(4, col, end, hy_sem.at[2 * end + (0 if end else up)], peer)
 
     def to_x(up, k, end):
         peer = gx_up if up else gx_down
         dst = (0 if up else 6) + k
-        return sides(3 + k, dst, end, hx_sem.at[end, 3 * up + k], peer)
+        return sides(3 + k, dst, end, hx_sem.at[end, 4 if k == 1 else 2 * up + k // 2], peer)
 
     def start(copies):
         for copy in copies:
             copy.start()
 
-    def got_y(up, end):
-        got_tiles(2 - end, hy_sem.at[end, up])
+    def got_y_own(up):
+        got_tiles(2, hy_sem.at[up])
+
+    def got_y_ends():
+        got_tiles(2, hy_sem.at[2])
+
+    def got_x_middle(end):
+        got_tiles(2 * (2 - end), hx_sem.at[end, 4])
 
     def got_x(up, k, end):
-        got_tiles(2 - end, hx_sem.at[end, 3 * up + k])
+        got_tiles(2 - end, hx_sem.at[end, 2 * up + k // 2])
 
     def got_inner(col):
-        got_tiles(1, hc_sem.at[col])
+        got_tiles(INNER.count(INNER[col]), hc_sem.at[INNER[col]])
 
     start(tiles(17 + c, 19 - 3 * c, 1, hz_sem, cross))
     pair_copy.start()
     for up in (1, 0):
-        start(to_y(up, 0))
+
+        @pl.when(zl != up)
+        def _():
+            start(to_y(up, 0))
+
+    for up in (1, 0):
         start(to_x(up, 1, 0))
     start(inner(4))
     rs_recv[q] = rs_send[q]
@@ -398,9 +410,9 @@
 
     def weave(one, two):
         done = 0
-        for i, step in enumerate(one):
+        for i, step in enumerate(one or [lambda: None]):
             step()
-            while done * len(one) < (i + 1) * len(two):
+            while done * max(len(one), 1) < (i + 1) * len(two):
                 two[done]()
                 done += 1
 
@@ -427,7 +439,14 @@
             tab_i[rows, cols] = sine_of_cycles(cycles).astype(BF16)
         return carry
 
-    lax.fori_loop(0, 8, table_block, 0)
+    lax.fori_loop(0, 4, table_block, 0)
+    for up in (1, 0):
+
+        @pl.when(zl == up)
+        def _():
+            start(to_y(up, 0))
+
+    lax.fori_loop(4, 8, table_block, 0)
 
     got_tiles(1, hz_sem)
     for up in (1, 0):
@@ -454,28 +473,32 @@
             z_peer((z + i) % NZ),
         ).start()
 
-    for up, k in ((1, 0), (0, 2)):
-        got_y(up, 0)
-        start(inner(3 + k))
-        start(to_x(1, k, 0))
-        start(to_x(0, k, 0))
-    for up, col in ((1, 1), (0, 7)):
-        got_x(up, 1, 0)
+    def onward(near):
+        for up, k in ((1, 0), (0, 2)):
+
+            @pl.when((zl == up) == near)
+            def _():
+                got_y_own(up)
+                start(inner(3 + k))
+                start(to_x(1, k, 0))
+                start(to_x(0, k, 0))
+
+    onward(True)
+    got_x_middle(0)
+    for col in (1, 7):
         start(inner(col))
-    for up, k in ((1, 0), (0, 2)):
-        got_y(up, 1)
+    onward(False)
+    got_x_middle(1)
+    got_inner(1)
+    weave(radial_steps(1, 0), [])
+    weave(radial_steps(7, 1), pool_steps(1, 0))
+    got_y_ends()
+    for k in (0, 2):
         start(to_x(1, k, 1))
         start(to_x(0, k, 1))
     got_inner(3)
-    weave(radial_steps(3, 0), [])
-    got_inner(5)
+    weave(radial_steps(3, 0), pool_steps(7, 1))
     weave(radial_steps(5, 1), pool_steps(3, 0))
-    got_x(1, 1, 1)
-    got_inner(1)
-    weave(radial_steps(1, 0), pool_steps(5, 1))
-    got_x(0, 1, 1)
-    got_inner(7)
-    weave(radial_steps(7, 1), pool_steps(1, 0))
     all_of(bytes_of, load_sem.at[4])
     mix_high = mix_ref[...].astype(BF16)
     mix_low = (mix_ref[...] - mix_high.astype(F32)).astype(BF16)
@@ -508,7 +531,7 @@
     for up, k, col in corners:
         got_x(up, k, 0)
         start(inner(col))
-    before = pool_steps(7, 1)
+    before = pool_steps(5, 1)
     for i, (up, k, col) in enumerate(corners):
         got_x(up, k, 1)
         got_inner(col)
@@ -530,19 +553,19 @@
     for i in (0, 1, 3, 2):
         some = ga_recv.at[pl.ds(i * 4, 4 if i else 3)]
         all_of(some, ga_sem.at[i])
-        cols = slice(i * 256, i * 256 + 256)
-        spectrum = ga_recv[i * 4 : i * 4 + 4].reshape(256, D)
         theirs = theirs + jnp.dot(
-            tab_i[2 * TILE :, cols], spectrum, preferred_element_type=F32
+            tab_i[2 * TILE :, i * 256 : i * 256 + 256],
+            ga_recv[i * 4 : i * 4 + 4].reshape(256, D),
+            preferred_element_type=F32,
         )
-    ls_send[...] = theirs
+    ls_send[...] = theirs.astype(BF16)
     last = remote(ls_send, ls_recv, coll_sem.at[5], coll_sem.at[6], partner)
     last.start()
     ours = far[...] + jnp.dot(
         tab_i[: 2 * TILE], ga_recv[...].reshape(K, D), preferred_element_type=F32
     )
     last.wait_recv()
-    summed = ours + ls_recv[...]
+    summed = ours + ls_recv[...].astype(F32)
     mean = jnp.mean(summed * summed, axis=-1, keepdims=True)
     normed = summed * lax.rsqrt(mean + EPS) * gain_ref[...]
     hidden = jnp.dot(normed.astype(BF16), up_ref[...], preferred_element_type=F32)
@@ -595,8 +618,8 @@
             vmem((NZ, 64, D), BF16),
             vmem((64, D), BF16),
             vmem((16, 64, D), BF16),
-            vmem((2 * TILE, D), F32),
-            vmem((2 * TILE, D), F32),
+            vmem((2 * TILE, D), BF16),
+            vmem((2 * TILE, D), BF16),
             vmem((16, K), F32),
             vmem((K, 16), BF16),
             vmem((4 * TILE, 16), BF16),
@@ -614,10 +637,10 @@
             dma((3,)),
             dma,
             dma,
-            dma((2, 2)),
-            dma((2, 6)),
-            dma((9,)),
-            dma((4,)),
+            dma((3,)),
+            dma((2, 5)),
+            dma((7,)),
+            dma,
             dma((7,)),
             dma((4,)),
             pltpu.SemaphoreType.REGULAR,

time: 31.6 us -> 31.4 us (level)
  no operation moved by 1% of the time
where the time goes in v5:
time: 31.4 us; the launch traced here: 31.3 us
  Pallas kernels  30.6 us (97%)
  local copies, waits for them, and re-layouts  0.63 us (2%)
    pallas_call x1, Pallas kernels, on_device(): pl.pallas_call(kernel, out_shape=pltpu.VMEM((2, TILE, D), BF16), in_specs...  30.6 us
    unnamed x1, local copies, waits for them, and re-layouts  0.63 us

profile of v5, /device:TPU:1, one launch (start us, length us, event | category | flops | bytes accessed | tf_op | source)
XLA Modules:
  0.0 31.3 jit_solution(7403751403994673002)
XLA Ops:
  0.0 30.6 %shard_map.100 = bf16[2,128,128]{2,1,0:T(8,128)(2,1)S(1)} custom-call(bf16[2,128,128]{2,1,0:T(8,128)(2,1)} %bitcast.5, s32[3,2,128]{2,1,0:T(2,128)} %bitcast.6, s32[3,1024]{1,0:T(4,128)} %wave_hbm.1, bf16[128,128]{1,0:T(8,128)(2,1)} %cw_hbm.1, f32[1024,128]{1,0:T(8,128)} %filt_hbm.1, f32[128,128]{1,0:T(8,128)} %mix_hbm.1, bf16[768,128]{1,0:T(8,128)(2,1)} %rmix_hbm.1, ...), custom_call_target="tpu_custom_call" | custom-call | tf_op jit(solution)/shard_map/pallas_call | solution.py:593
  30.6 0.6 %copy.12 = bf16[1,1,2,128,128]{4,3,2,1,0:T(8,128)(2,1)} copy(bf16[1,1,2,128,128]{4,3,2,1,0:T(8,128)(2,1)S(1)} %bitcast.4) | data formatting | bytes 131072

commit v6 on v5

--- a/solution.py
+++ b/solution.py
@@ -28,7 +28,9 @@
     -12.271259128462068,
 )
 ORDER = (2, 1, 3, 0)
-PLANE = [(i, j) for i in ORDER for j in ORDER if i or j]
+ALONG = [(i, j) for i in (2, 1) for j in ORDER]
+BACK = [(3, 2), (0, 2), (3, 1), (0, 1), (3, 3), (0, 3), (3, 0)]
+PLANE = [step for pair in zip(ALONG, BACK) for step in pair] + ALONG[7:]
 INNER = (3, 2, 4, 1, 0, 1, 5, 2, 6)
 LINE = sorted(range(1, 8), key=lambda i: -min(i, 8 - i))
 FIRST = (((0,), (0,)), ((), ()))
@@ -332,8 +334,6 @@
         def _():
             start(to_y(up, 0))
 
-    for up in (1, 0):
-        start(to_x(up, 1, 0))
     start(inner(4))
     rs_recv[q] = rs_send[q]
 
@@ -446,6 +446,8 @@
         def _():
             start(to_y(up, 0))
 
+    for up in (1, 0):
+        start(to_x(up, 1, 0))
     lax.fori_loop(4, 8, table_block, 0)
 
     got_tiles(1, hz_sem)

time: 31.4 us -> 31 us (0.987)
    pallas_call x1, Pallas kernels: 30.6 us -> 30.3 us  [on_device(): pl.pallas_call(kernel, out_shape=pltpu.VMEM((2, TILE, D), BF16), in_specs...]
where the time goes in v6:
time: 31 us; the launch traced here: 30.9 us
  Pallas kernels  30.3 us (98%)
  local copies, waits for them, and re-layouts  0.63 us (2%)
    pallas_call x1, Pallas kernels, on_device(): pl.pallas_call(kernel, out_shape=pltpu.VMEM((2, TILE, D), BF16), in_specs...  30.3 us
    unnamed x1, local copies, waits for them, and re-layouts  0.63 us

profile of v6, /device:TPU:1, one launch (start us, length us, event | category | flops | bytes accessed | tf_op | source)
XLA Modules:
  0.0 30.9 jit_solution(18344945610905459969)
XLA Ops:
  0.0 30.3 %shard_map.100 = bf16[2,128,128]{2,1,0:T(8,128)(2,1)S(1)} custom-call(bf16[2,128,128]{2,1,0:T(8,128)(2,1)} %bitcast.5, s32[3,2,128]{2,1,0:T(2,128)} %bitcast.6, s32[3,1024]{1,0:T(4,128)} %wave_hbm.1, bf16[128,128]{1,0:T(8,128)(2,1)} %cw_hbm.1, f32[1024,128]{1,0:T(8,128)} %filt_hbm.1, f32[128,128]{1,0:T(8,128)} %mix_hbm.1, bf16[768,128]{1,0:T(8,128)(2,1)} %rmix_hbm.1, ...), custom_call_target="tpu_custom_call" | custom-call | tf_op jit(solution)/shard_map/pallas_call | solution.py:595
  30.3 0.6 %copy.12 = bf16[1,1,2,128,128]{4,3,2,1,0:T(8,128)(2,1)} copy(bf16[1,1,2,128,128]{4,3,2,1,0:T(8,128)(2,1)S(1)} %bitcast.4) | data formatting | bytes 131072

commit v7 on v6

--- a/solution.py
+++ b/solution.py
@@ -126,8 +126,11 @@
     def at(gx_, gy_, gz_):
         return {"gx": gx_, "gy": gy_, "gz": gz_}
 
+    def turn(i):
+        return (4 - i) % 4 * c + i * (1 - c)
+
     def plane_peer(i, j):
-        x_, y_ = (gx + i) % NX, (y + j) % NY
+        x_, y_ = (gx + turn(i)) % NX, (y + turn(j)) % NY
         return x_ * NY + y_, at(x_, y_ * 2 + zl, gz)
 
     def z_peer(i):
@@ -501,6 +504,17 @@
     got_inner(3)
     weave(radial_steps(3, 0), pool_steps(7, 1))
     weave(radial_steps(5, 1), pool_steps(3, 0))
+    corners = ((1, 0, 0), (1, 2, 2), (0, 0, 6), (0, 2, 8))
+
+    def relay(near):
+        for up, k, col in corners:
+
+            @pl.when((zl == 1 - k // 2) == near)
+            def _():
+                got_x(up, k, 0)
+                start(inner(col))
+
+    relay(True)
     all_of(bytes_of, load_sem.at[4])
     mix_high = mix_ref[...].astype(BF16)
     mix_low = (mix_ref[...] - mix_high.astype(F32)).astype(BF16)
@@ -520,19 +534,16 @@
     ga_send[...] = block
 
     for i, j in PLANE:
-        back = (4 - i) % 4
+        back = (4 - turn(i)) % 4
         remote(
             ga_send,
-            ga_recv.at[back * 4 + (4 - j) % 4],
+            ga_recv.at[back * 4 + (4 - turn(j)) % 4],
             coll_sem.at[4],
             ga_sem.at[back],
             plane_peer(i, j)[1],
         ).start()
     ga_recv[0] = block
-    corners = ((1, 0, 0), (1, 2, 2), (0, 0, 6), (0, 2, 8))
-    for up, k, col in corners:
-        got_x(up, k, 0)
-        start(inner(col))
+    relay(False)
     before = pool_steps(5, 1)
     for i, (up, k, col) in enumerate(corners):
         got_x(up, k, 1)

time: 31 us -> 31.2 us (level)
  no operation moved by 1% of the time
where the time goes in v7:
time: 31.2 us; the launch traced here: 31.1 us
  Pallas kernels  30.5 us (98%)
  local copies, waits for them, and re-layouts  0.63 us (2%)
    pallas_call x1, Pallas kernels, on_device(): pl.pallas_call(kernel, out_shape=pltpu.VMEM((2, TILE, D), BF16), in_specs...  30.5 us
    unnamed x1, local copies, waits for them, and re-layouts  0.63 us

profile of v7, /device:TPU:1, one launch (start us, length us, event | category | flops | bytes accessed | tf_op | source)
XLA Modules:
  0.0 31.1 jit_solution(10874485909151552287)
XLA Ops:
  0.0 30.5 %shard_map.100 = bf16[2,128,128]{2,1,0:T(8,128)(2,1)S(1)} custom-call(bf16[2,128,128]{2,1,0:T(8,128)(2,1)} %bitcast.5, s32[3,2,128]{2,1,0:T(2,128)} %bitcast.6, s32[3,1024]{1,0:T(4,128)} %wave_hbm.1, bf16[128,128]{1,0:T(8,128)(2,1)} %cw_hbm.1, f32[1024,128]{1,0:T(8,128)} %filt_hbm.1, f32[128,128]{1,0:T(8,128)} %mix_hbm.1, bf16[768,128]{1,0:T(8,128)(2,1)} %rmix_hbm.1, ...), custom_call_target="tpu_custom_call" | custom-call | tf_op jit(solution)/shard_map/pallas_call | solution.py:606
  30.5 0.6 %copy.12 = bf16[1,1,2,128,128]{4,3,2,1,0:T(8,128)(2,1)} copy(bf16[1,1,2,128,128]{4,3,2,1,0:T(8,128)(2,1)S(1)} %bitcast.4) | data formatting | bytes 131072
